TPU v7x, 768 devices: a whole 4x8x12 slice. The times are simulated.
768 devices in a mesh: lat: 48 (over z, y_hi), lon: 16 (over y_lo, x, core).
Axes of the slice: x: 4, y: 8 (y_hi: 4, y_lo: 2; y = y_hi * 2 + y_lo), z: 12, core: 2. Of those that a mesh axis runs over, the one named last changes fastest.
Arguments:
- initial_state: float32 [6, 2304, 2048], P(None, 'lat', 'lon'), may hold values from -6 to 6
- source: float32 [6, 2304, 2048], P(None, 'lat', 'lon'), may hold values from -3 to 3
- cotangent: float32 [6, 2304, 2048], P(None, 'lat', 'lon'), may hold values from -6 to 6
- face_coefs: float32 [2, 2304, 2048], P(None, 'lat', 'lon'), may hold values from 0.03 to 0.1
- land_mask: int32 [6, 2304, 2048], P(None, 'lat', 'lon'), may hold values 0 or 1
- bottom: int32 [2304, 2048], P('lat', 'lon'), may hold values from 1 to 6
Outputs:
- final_state: float32 [6, 2304, 2048], P(None, 'lat', 'lon')
- grad_initial: float32 [6, 2304, 2048], P(None, 'lat', 'lon')
- grad_source: float32 [6, 2304, 2048], P(None, 'lat', 'lon')
All inputs are finite; a program needn't handle non-finite values. No bound on the sum of `land_mask` on one device may be relied on, other than what follows from the above.
Results may differ from a plain program's by a relative error of at most 0.00002.
Values sent between devices are 32-bit elements; how exact they have to be, the bound alone decides.
A program may use at most 32 MiB of HBM per device.

v0:
```python
import jax
import jax.numpy as jnp
from jax import lax
from jax.sharding import PartitionSpec as P

STEPS = 4


vertical_coef = 0.04


def padded_2(cells, sides, width):
    for axis, dim in sides:
        count = lax.axis_size(axis)
        head = lax.slice_in_dim(cells, 0, width, axis=dim)
        tail = lax.slice_in_dim(cells, cells.shape[dim] - width, cells.shape[dim], axis=dim)
        cells = jnp.concatenate(
            [
                lax.ppermute(tail, axis, [(i, (i + 1) % count) for i in range(count)]),
                cells,
                lax.ppermute(head, axis, [((i + 1) % count, i) for i in range(count)]),
            ],
            axis=dim,
        )
    return cells


def operate(padded, wet_mask, coef_lon, coef_lat):
    flux_east = (
        coef_lon[None, :, :-1]
        * (wet_mask[:, :, :-1] * wet_mask[:, :, 1:])
        * (padded[:, :, 1:] - padded[:, :, :-1])
    )
    flux_north = (
        coef_lat[None, :-1, :]
        * (wet_mask[:, :-1, :] * wet_mask[:, 1:, :])
        * (padded[:, 1:, :] - padded[:, :-1, :])
    )
    center = padded[:, 1:-1, 1:-1]
    wet_center = wet_mask[:, 1:-1, 1:-1]
    flux_up = vertical_coef * (wet_center[:-1] * wet_center[1:]) * (center[1:] - center[:-1])
    zero_level = jnp.zeros_like(center[:1])
    vertical = jnp.concatenate([flux_up, zero_level], 0) - jnp.concatenate([zero_level, flux_up], 0)
    east_part = flux_east[:, 1:-1, 1:] - flux_east[:, 1:-1, :-1]
    north_part = flux_north[:, 1:, 1:-1] - flux_north[:, :-1, 1:-1]
    return center + east_part + north_part + vertical


def body(initial_state, source, cotangent, face_coefs, land_mask, bottom):
    levels = lax.broadcasted_iota(jnp.int32, land_mask.shape, 0)
    wet_mask = jnp.where(levels < bottom[None, :, :], land_mask, 0).astype(jnp.float32)
    tile_rows = face_coefs.shape[1]
    global_rows = lax.axis_index("lat") * tile_rows + lax.broadcasted_iota(
        jnp.int32, face_coefs.shape[1:], 0
    )
    lat_open = global_rows < tile_rows * lax.axis_size("lat") - 1
    coef_pair = jnp.stack([face_coefs[0], jnp.where(lat_open, face_coefs[1], jnp.float32(0.0))])
    grad_source = jnp.zeros_like(source)
    coef_wide, wet_wide = (
        padded_2(coef_pair, (("lat", 1), ("lon", 2)), 1),
        padded_2(wet_mask, (("lat", 1), ("lon", 2)), 1),
    )

    def extend(values):
        return padded_2(values, (("lat", 1), ("lon", 2)), 1)

    tracer = initial_state
    curves = []
    for step_index in range(STEPS):
        bounded = jnp.tanh(operate(extend(tracer), wet_wide, coef_wide[0], coef_wide[1]))
        curves.append(bounded)
        tracer = wet_mask * (bounded + source)
    adjoint = cotangent
    for bounded in reversed(curves):
        grad_source = grad_source + wet_mask * adjoint
        inner_adjoint = wet_mask * (1.0 - bounded * bounded) * adjoint
        adjoint = operate(extend(inner_adjoint), wet_wide, coef_wide[0], coef_wide[1])
    return (tracer, adjoint, grad_source)


def solution(mesh):
    return jax.shard_map(
        body,
        mesh=mesh,
        in_specs=(
            P(None, "lat", "lon"),
            P(None, "lat", "lon"),
            P(None, "lat", "lon"),
            P(None, "lat", "lon"),
            P(None, "lat", "lon"),
            P("lat", "lon"),
        ),
        out_specs=(P(None, "lat", "lon"), P(None, "lat", "lon"), P(None, "lat", "lon")),
        check_vma=False,
    )
```

profile of v0, /device:TPU:1, one launch (start us, length us, event | category | flops | bytes accessed | tf_op | source)
XLA Modules:
  0.0 233.2 jit_solution(17475553803703115408)
XLA Ops:
  1.5 5.0 %collective-permute-start = (f32[2,1,128]{2,1,0:T(1,128)S(1)}, f32[2,1,128]{2,1,0:T(1,128)S(1)}, u32[]{:S(2)}, u32[]{:S(2)}) collective-permute-start(f32[2,1,128]{2,1,0:T(1,128)S(1)} %get-tuple-element.63), channel_id=1, source_target_pairs={{0,16},{16,32},{32,48},{48,64},{64,80},{80,96},{96,112},{112,128},... | collective-permute-start | bytes 3080 | tf_op jit(solution)/shard_map/ppermute | solution.py:19
  6.6 15.8 %collective-permute-start.1 = (f32[2,1,128]{2,1,0:T(1,128)S(1)}, f32[2,1,128]{2,1,0:T(1,128)S(1)}, u32[]{:S(2)}, u32[]{:S(2)}) collective-permute-start(f32[2,1,128]{2,1,0:T(1,128)S(1)} %get-tuple-element.64), channel_id=1, source_target_pairs={{16,0},{32,16},{48,32},{64,48},{80,64},{96,80},{112,96},{128,112},... | collective-permute-start | bytes 3080 | tf_op jit(solution)/shard_map/ppermute | solution.py:21
  25.1 7.6 %collective-permute-start.5 = (f32[6,1,128]{2,1,0:T(1,128)S(1)}, f32[6,1,128]{2,1,0:T(1,128)S(1)}, u32[]{:S(2)}, u32[]{:S(2)}) collective-permute-start(f32[6,1,128]{2,1,0:T(1,128)S(1)} %get-tuple-element.58), channel_id=1, source_target_pairs={{16,0},{32,16},{48,32},{64,48},{80,64},{96,80},{112,96},{128,112},... | collective-permute-start | bytes 9224 | tf_op jit(solution)/shard_map/ppermute | solution.py:21
  34.8 4.5 %collective-permute-start.2 = (f32[2,50,1]{2,1,0:T(8,128)S(1)}, f32[2,50,1]{2,1,0:T(8,128)S(1)}, u32[]{:S(2)}, u32[]{:S(2)}) collective-permute-start(f32[2,50,1]{2,1,0:T(8,128)S(1)} %get-tuple-element.61), channel_id=1, source_target_pairs={{0,1},{1,2},{2,3},{3,4},{4,5},{5,6},{6,7},{7,8},{8,9},{9,10},{10,1... | collective-permute-start | bytes 1208 | tf_op jit(solution)/shard_map/ppermute | solution.py:19
  41.3 7.9 %collective-permute-start.9 = (f32[6,1,128]{2,1,0:T(1,128)S(1)}, f32[6,1,128]{2,1,0:T(1,128)S(1)}, u32[]{:S(2)}, u32[]{:S(2)}) collective-permute-start(f32[6,1,128]{2,1,0:T(1,128)S(1)} %get-tuple-element.60), channel_id=1, source_target_pairs={{16,0},{32,16},{48,32},{64,48},{80,64},{96,80},{112,96},{128,112},... | collective-permute-start | bytes 9224 | tf_op jit(solution)/shard_map/ppermute | solution.py:21
  49.5 3.9 %collective-permute-start.6 = (f32[6,50,1]{2,1,0:T(8,128)S(1)}, f32[6,50,1]{2,1,0:T(8,128)S(1)}, u32[]{:S(2)}, u32[]{:S(2)}) collective-permute-start(f32[6,50,1]{2,1,0:T(8,128)S(1)} %get-tuple-element.37), channel_id=1, source_target_pairs={{0,1},{1,2},{2,3},{3,4},{4,5},{5,6},{6,7},{7,8},{8,9},{9,10},{10,1... | collective-permute-start | bytes 3608 | tf_op jit(solution)/shard_map/ppermute | solution.py:19
  53.4 2.9 %collective-permute-start.7 = (f32[6,50,1]{2,1,0:T(8,128)S(1)}, f32[6,50,1]{2,1,0:T(8,128)S(1)}, u32[]{:S(2)}, u32[]{:S(2)}) collective-permute-start(f32[6,50,1]{2,1,0:T(8,128)S(1)} %get-tuple-element.38), channel_id=1, source_target_pairs={{1,0},{2,1},{3,2},{4,3},{5,4},{6,5},{7,6},{8,7},{9,8},{10,9},{11,1... | collective-permute-start | bytes 3608 | tf_op jit(solution)/shard_map/ppermute | solution.py:21
  56.5 5.8 %collective-permute-start.10 = (f32[6,50,1]{2,1,0:T(8,128)S(1)}, f32[6,50,1]{2,1,0:T(8,128)S(1)}, u32[]{:S(2)}, u32[]{:S(2)}) collective-permute-start(f32[6,50,1]{2,1,0:T(8,128)S(1)} %get-tuple-element.40), channel_id=1, source_target_pairs={{1,0},{2,1},{3,2},{4,3},{5,4},{6,5},{7,6},{8,7},{9,8},{10,9},{11,1... | collective-permute-start | bytes 3608 | tf_op jit(solution)/shard_map/ppermute | solution.py:21
  69.9 7.6 %collective-permute-start.13 = (f32[6,1,128]{2,1,0:T(1,128)S(1)}, f32[6,1,128]{2,1,0:T(1,128)S(1)}, u32[]{:S(2)}, u32[]{:S(2)}) collective-permute-start(f32[6,1,128]{2,1,0:T(1,128)S(1)} %get-tuple-element.56), channel_id=1, source_target_pairs={{16,0},{32,16},{48,32},{64,48},{80,64},{96,80},{112,96},{128,112},... | collective-permute-start | bytes 9224 | tf_op jit(solution)/shard_map/ppermute | solution.py:21
  78.4 7.7 %collective-permute-start.14 = (f32[6,50,1]{2,1,0:T(8,128)S(1)}, f32[6,50,1]{2,1,0:T(8,128)S(1)}, u32[]{:S(2)}, u32[]{:S(2)}) collective-permute-start(f32[6,50,1]{2,1,0:T(8,128)S(1)} %get-tuple-element.36), channel_id=1, source_target_pairs={{1,0},{2,1},{3,2},{4,3},{5,4},{6,5},{7,6},{8,7},{9,8},{10,9},{11,1... | collective-permute-start | bytes 3608 | tf_op jit(solution)/shard_map/ppermute | solution.py:21
  88.0 2.3 collective-permute-done.15
  93.0 8.1 %collective-permute-start.17 = (f32[6,1,128]{2,1,0:T(1,128)S(1)}, f32[6,1,128]{2,1,0:T(1,128)S(1)}, u32[]{:S(2)}, u32[]{:S(2)}) collective-permute-start(f32[6,1,128]{2,1,0:T(1,128)S(1)} %get-tuple-element.54), channel_id=1, source_target_pairs={{16,0},{32,16},{48,32},{64,48},{80,64},{96,80},{112,96},{128,112},... | collective-permute-start | bytes 9224 | tf_op jit(solution)/shard_map/ppermute | solution.py:21
  101.9 7.4 %collective-permute-start.18 = (f32[6,50,1]{2,1,0:T(8,128)S(1)}, f32[6,50,1]{2,1,0:T(8,128)S(1)}, u32[]{:S(2)}, u32[]{:S(2)}) collective-permute-start(f32[6,50,1]{2,1,0:T(8,128)S(1)} %get-tuple-element.34), channel_id=1, source_target_pairs={{1,0},{2,1},{3,2},{4,3},{5,4},{6,5},{7,6},{8,7},{9,8},{10,9},{11,1... | collective-permute-start | bytes 3608 | tf_op jit(solution)/shard_map/ppermute | solution.py:21
  111.3 2.3 collective-permute-done.19
  116.2 8.1 %collective-permute-start.21 = (f32[6,1,128]{2,1,0:T(1,128)S(1)}, f32[6,1,128]{2,1,0:T(1,128)S(1)}, u32[]{:S(2)}, u32[]{:S(2)}) collective-permute-start(f32[6,1,128]{2,1,0:T(1,128)S(1)} %get-tuple-element.52), channel_id=1, source_target_pairs={{16,0},{32,16},{48,32},{64,48},{80,64},{96,80},{112,96},{128,112},... | collective-permute-start | bytes 9224 | tf_op jit(solution)/shard_map/ppermute | solution.py:21
  125.2 7.4 %collective-permute-start.22 = (f32[6,50,1]{2,1,0:T(8,128)S(1)}, f32[6,50,1]{2,1,0:T(8,128)S(1)}, u32[]{:S(2)}, u32[]{:S(2)}) collective-permute-start(f32[6,50,1]{2,1,0:T(8,128)S(1)} %get-tuple-element.32), channel_id=1, source_target_pairs={{1,0},{2,1},{3,2},{4,3},{5,4},{6,5},{7,6},{8,7},{9,8},{10,9},{11,1... | collective-permute-start | bytes 3608 | tf_op jit(solution)/shard_map/ppermute | solution.py:21
  140.1 8.1 %collective-permute-start.25 = (f32[6,1,128]{2,1,0:T(1,128)S(1)}, f32[6,1,128]{2,1,0:T(1,128)S(1)}, u32[]{:S(2)}, u32[]{:S(2)}) collective-permute-start(f32[6,1,128]{2,1,0:T(1,128)S(1)} %get-tuple-element.50), channel_id=1, source_target_pairs={{16,0},{32,16},{48,32},{64,48},{80,64},{96,80},{112,96},{128,112},... | collective-permute-start | bytes 9224 | tf_op jit(solution)/shard_map/ppermute | solution.py:21
  149.1 7.4 %collective-permute-start.26 = (f32[6,50,1]{2,1,0:T(8,128)S(1)}, f32[6,50,1]{2,1,0:T(8,128)S(1)}, u32[]{:S(2)}, u32[]{:S(2)}) collective-permute-start(f32[6,50,1]{2,1,0:T(8,128)S(1)} %get-tuple-element.30), channel_id=1, source_target_pairs={{1,0},{2,1},{3,2},{4,3},{5,4},{6,5},{7,6},{8,7},{9,8},{10,9},{11,1... | collective-permute-start | bytes 3608 | tf_op jit(solution)/shard_map/ppermute | solution.py:21
  163.4 8.1 %collective-permute-start.29 = (f32[6,1,128]{2,1,0:T(1,128)S(1)}, f32[6,1,128]{2,1,0:T(1,128)S(1)}, u32[]{:S(2)}, u32[]{:S(2)}) collective-permute-start(f32[6,1,128]{2,1,0:T(1,128)S(1)} %get-tuple-element.48), channel_id=1, source_target_pairs={{16,0},{32,16},{48,32},{64,48},{80,64},{96,80},{112,96},{128,112},... | collective-permute-start | bytes 9224 | tf_op jit(solution)/shard_map/ppermute | solution.py:21
  172.4 7.4 %collective-permute-start.30 = (f32[6,50,1]{2,1,0:T(8,128)S(1)}, f32[6,50,1]{2,1,0:T(8,128)S(1)}, u32[]{:S(2)}, u32[]{:S(2)}) collective-permute-start(f32[6,50,1]{2,1,0:T(8,128)S(1)} %get-tuple-element.28), channel_id=1, source_target_pairs={{1,0},{2,1},{3,2},{4,3},{5,4},{6,5},{7,6},{8,7},{9,8},{10,9},{11,1... | collective-permute-start | bytes 3608 | tf_op jit(solution)/shard_map/ppermute | solution.py:21
  186.6 8.1 %collective-permute-start.33 = (f32[6,1,128]{2,1,0:T(1,128)S(1)}, f32[6,1,128]{2,1,0:T(1,128)S(1)}, u32[]{:S(2)}, u32[]{:S(2)}) collective-permute-start(f32[6,1,128]{2,1,0:T(1,128)S(1)} %get-tuple-element.46), channel_id=1, source_target_pairs={{16,0},{32,16},{48,32},{64,48},{80,64},{96,80},{112,96},{128,112},... | collective-permute-start | bytes 9224 | tf_op jit(solution)/shard_map/ppermute | solution.py:21
  195.6 7.4 %collective-permute-start.34 = (f32[6,50,1]{2,1,0:T(8,128)S(1)}, f32[6,50,1]{2,1,0:T(8,128)S(1)}, u32[]{:S(2)}, u32[]{:S(2)}) collective-permute-start(f32[6,50,1]{2,1,0:T(8,128)S(1)} %get-tuple-element.26), channel_id=1, source_target_pairs={{1,0},{2,1},{3,2},{4,3},{5,4},{6,5},{7,6},{8,7},{9,8},{10,9},{11,1... | collective-permute-start | bytes 3608 | tf_op jit(solution)/shard_map/ppermute | solution.py:21
  211.2 8.1 %collective-permute-start.37 = (f32[6,1,128]{2,1,0:T(1,128)S(1)}, f32[6,1,128]{2,1,0:T(1,128)S(1)}, u32[]{:S(2)}, u32[]{:S(2)}) collective-permute-start(f32[6,1,128]{2,1,0:T(1,128)S(1)} %get-tuple-element.42), channel_id=1, source_target_pairs={{16,0},{32,16},{48,32},{64,48},{80,64},{96,80},{112,96},{128,112},... | collective-permute-start | bytes 9224 | tf_op jit(solution)/shard_map/ppermute | solution.py:21
  220.2 7.4 %collective-permute-start.38 = (f32[6,50,1]{2,1,0:T(8,128)S(1)}, f32[6,50,1]{2,1,0:T(8,128)S(1)}, u32[]{:S(2)}, u32[]{:S(2)}) collective-permute-start(f32[6,50,1]{2,1,0:T(8,128)S(1)} %get-tuple-element.24), channel_id=1, source_target_pairs={{1,0},{2,1},{3,2},{4,3},{5,4},{6,5},{7,6},{8,7},{9,8},{10,9},{11,1... | collective-permute-start | bytes 3608 | tf_op jit(solution)/shard_map/ppermute | solution.py:21
  (144 shorter events, 65.3 us)
Async XLA Ops:
  1.5 33.2 %collective-permute-start = (f32[2,1,128]{2,1,0:T(1,128)S(1)}, f32[2,1,128]{2,1,0:T(1,128)S(1)}, u32[]{:S(2)}, u32[]{:S(2)}) collective-permute-start(f32[2,1,128]{2,1,0:T(1,128)S(1)} %get-tuple-element.63), channel_id=1, source_target_pairs={{0,16},{16,32},{32,48},{48,64},{64,80},{80,96},{96,112},{112,128},... | collective-permute-start | bytes 3080 | tf_op jit(solution)/shard_map/ppermute | solution.py:19
  6.6 28.1 %collective-permute-start.1 = (f32[2,1,128]{2,1,0:T(1,128)S(1)}, f32[2,1,128]{2,1,0:T(1,128)S(1)}, u32[]{:S(2)}, u32[]{:S(2)}) collective-permute-start(f32[2,1,128]{2,1,0:T(1,128)S(1)} %get-tuple-element.64), channel_id=1, source_target_pairs={{16,0},{32,16},{48,32},{64,48},{80,64},{96,80},{112,96},{128,112},... | collective-permute-start | bytes 3080 | tf_op jit(solution)/shard_map/ppermute | solution.py:21
  23.2 26.1 %collective-permute-start.4 = (f32[6,1,128]{2,1,0:T(1,128)S(1)}, f32[6,1,128]{2,1,0:T(1,128)S(1)}, u32[]{:S(2)}, u32[]{:S(2)}) collective-permute-start(f32[6,1,128]{2,1,0:T(1,128)S(1)} %get-tuple-element.57), channel_id=1, source_target_pairs={{0,16},{16,32},{32,48},{48,64},{64,80},{80,96},{96,112},{112,128},... | collective-permute-start | bytes 9224 | tf_op jit(solution)/shard_map/ppermute | solution.py:19
  25.1 24.2 %collective-permute-start.5 = (f32[6,1,128]{2,1,0:T(1,128)S(1)}, f32[6,1,128]{2,1,0:T(1,128)S(1)}, u32[]{:S(2)}, u32[]{:S(2)}) collective-permute-start(f32[6,1,128]{2,1,0:T(1,128)S(1)} %get-tuple-element.58), channel_id=1, source_target_pairs={{16,0},{32,16},{48,32},{64,48},{80,64},{96,80},{112,96},{128,112},... | collective-permute-start | bytes 9224 | tf_op jit(solution)/shard_map/ppermute | solution.py:21
  32.8 23.6 %collective-permute-start.8 = (f32[6,1,128]{2,1,0:T(1,128)S(1)}, f32[6,1,128]{2,1,0:T(1,128)S(1)}, u32[]{:S(2)}, u32[]{:S(2)}) collective-permute-start(f32[6,1,128]{2,1,0:T(1,128)S(1)} %get-tuple-element.59), channel_id=1, source_target_pairs={{0,16},{16,32},{32,48},{48,64},{64,80},{80,96},{96,112},{112,128},... | collective-permute-start | bytes 9224 | tf_op jit(solution)/shard_map/ppermute | solution.py:19
  39.3 9.8 %collective-permute-start.3 = (f32[2,50,1]{2,1,0:T(8,128)S(1)}, f32[2,50,1]{2,1,0:T(8,128)S(1)}, u32[]{:S(2)}, u32[]{:S(2)}) collective-permute-start(f32[2,50,1]{2,1,0:T(8,128)S(1)} %get-tuple-element.62), channel_id=1, source_target_pairs={{1,0},{2,1},{3,2},{4,3},{5,4},{6,5},{7,6},{8,7},{9,8},{10,9},{11,1... | collective-permute-start | bytes 1208 | tf_op jit(solution)/shard_map/ppermute | solution.py:21
  41.3 15.1 %collective-permute-start.9 = (f32[6,1,128]{2,1,0:T(1,128)S(1)}, f32[6,1,128]{2,1,0:T(1,128)S(1)}, u32[]{:S(2)}, u32[]{:S(2)}) collective-permute-start(f32[6,1,128]{2,1,0:T(1,128)S(1)} %get-tuple-element.60), channel_id=1, source_target_pairs={{16,0},{32,16},{48,32},{64,48},{80,64},{96,80},{112,96},{128,112},... | collective-permute-start | bytes 9224 | tf_op jit(solution)/shard_map/ppermute | solution.py:21
  49.5 14.7 %collective-permute-start.6 = (f32[6,50,1]{2,1,0:T(8,128)S(1)}, f32[6,50,1]{2,1,0:T(8,128)S(1)}, u32[]{:S(2)}, u32[]{:S(2)}) collective-permute-start(f32[6,50,1]{2,1,0:T(8,128)S(1)} %get-tuple-element.37), channel_id=1, source_target_pairs={{0,1},{1,2},{2,3},{3,4},{4,5},{5,6},{6,7},{7,8},{8,9},{9,10},{10,1... | collective-permute-start | bytes 3608 | tf_op jit(solution)/shard_map/ppermute | solution.py:19
  53.4 10.8 %collective-permute-start.7 = (f32[6,50,1]{2,1,0:T(8,128)S(1)}, f32[6,50,1]{2,1,0:T(8,128)S(1)}, u32[]{:S(2)}, u32[]{:S(2)}) collective-permute-start(f32[6,50,1]{2,1,0:T(8,128)S(1)} %get-tuple-element.38), channel_id=1, source_target_pairs={{1,0},{2,1},{3,2},{4,3},{5,4},{6,5},{7,6},{8,7},{9,8},{10,9},{11,1... | collective-permute-start | bytes 3608 | tf_op jit(solution)/shard_map/ppermute | solution.py:21
  68.0 9.5 %collective-permute-start.12 = (f32[6,1,128]{2,1,0:T(1,128)S(1)}, f32[6,1,128]{2,1,0:T(1,128)S(1)}, u32[]{:S(2)}, u32[]{:S(2)}) collective-permute-start(f32[6,1,128]{2,1,0:T(1,128)S(1)} %get-tuple-element.55), channel_id=1, source_target_pairs={{0,16},{16,32},{32,48},{48,64},{64,80},{80,96},{96,112},{112,128},... | collective-permute-start | bytes 9224 | tf_op jit(solution)/shard_map/ppermute | solution.py:19
  78.4 9.6 %collective-permute-start.14 = (f32[6,50,1]{2,1,0:T(8,128)S(1)}, f32[6,50,1]{2,1,0:T(8,128)S(1)}, u32[]{:S(2)}, u32[]{:S(2)}) collective-permute-start(f32[6,50,1]{2,1,0:T(8,128)S(1)} %get-tuple-element.36), channel_id=1, source_target_pairs={{1,0},{2,1},{3,2},{4,3},{5,4},{6,5},{7,6},{8,7},{9,8},{10,9},{11,1... | collective-permute-start | bytes 3608 | tf_op jit(solution)/shard_map/ppermute | solution.py:21
  91.0 10.1 %collective-permute-start.16 = (f32[6,1,128]{2,1,0:T(1,128)S(1)}, f32[6,1,128]{2,1,0:T(1,128)S(1)}, u32[]{:S(2)}, u32[]{:S(2)}) collective-permute-start(f32[6,1,128]{2,1,0:T(1,128)S(1)} %get-tuple-element.53), channel_id=1, source_target_pairs={{0,16},{16,32},{32,48},{48,64},{64,80},{80,96},{96,112},{112,128},... | collective-permute-start | bytes 9224 | tf_op jit(solution)/shard_map/ppermute | solution.py:19
  93.0 8.9 %collective-permute-start.17 = (f32[6,1,128]{2,1,0:T(1,128)S(1)}, f32[6,1,128]{2,1,0:T(1,128)S(1)}, u32[]{:S(2)}, u32[]{:S(2)}) collective-permute-start(f32[6,1,128]{2,1,0:T(1,128)S(1)} %get-tuple-element.54), channel_id=1, source_target_pairs={{16,0},{32,16},{48,32},{64,48},{80,64},{96,80},{112,96},{128,112},... | collective-permute-start | bytes 9224 | tf_op jit(solution)/shard_map/ppermute | solution.py:21
  101.9 9.3 %collective-permute-start.18 = (f32[6,50,1]{2,1,0:T(8,128)S(1)}, f32[6,50,1]{2,1,0:T(8,128)S(1)}, u32[]{:S(2)}, u32[]{:S(2)}) collective-permute-start(f32[6,50,1]{2,1,0:T(8,128)S(1)} %get-tuple-element.34), channel_id=1, source_target_pairs={{1,0},{2,1},{3,2},{4,3},{5,4},{6,5},{7,6},{8,7},{9,8},{10,9},{11,1... | collective-permute-start | bytes 3608 | tf_op jit(solution)/shard_map/ppermute | solution.py:21
  114.3 10.1 %collective-permute-start.20 = (f32[6,1,128]{2,1,0:T(1,128)S(1)}, f32[6,1,128]{2,1,0:T(1,128)S(1)}, u32[]{:S(2)}, u32[]{:S(2)}) collective-permute-start(f32[6,1,128]{2,1,0:T(1,128)S(1)} %get-tuple-element.51), channel_id=1, source_target_pairs={{0,16},{16,32},{32,48},{48,64},{64,80},{80,96},{96,112},{112,128},... | collective-permute-start | bytes 9224 | tf_op jit(solution)/shard_map/ppermute | solution.py:19
  125.2 9.3 %collective-permute-start.22 = (f32[6,50,1]{2,1,0:T(8,128)S(1)}, f32[6,50,1]{2,1,0:T(8,128)S(1)}, u32[]{:S(2)}, u32[]{:S(2)}) collective-permute-start(f32[6,50,1]{2,1,0:T(8,128)S(1)} %get-tuple-element.32), channel_id=1, source_target_pairs={{1,0},{2,1},{3,2},{4,3},{5,4},{6,5},{7,6},{8,7},{9,8},{10,9},{11,1... | collective-permute-start | bytes 3608 | tf_op jit(solution)/shard_map/ppermute | solution.py:21
  138.2 10.1 %collective-permute-start.24 = (f32[6,1,128]{2,1,0:T(1,128)S(1)}, f32[6,1,128]{2,1,0:T(1,128)S(1)}, u32[]{:S(2)}, u32[]{:S(2)}) collective-permute-start(f32[6,1,128]{2,1,0:T(1,128)S(1)} %get-tuple-element.49), channel_id=1, source_target_pairs={{0,16},{16,32},{32,48},{48,64},{64,80},{80,96},{96,112},{112,128},... | collective-permute-start | bytes 9224 | tf_op jit(solution)/shard_map/ppermute | solution.py:19
  149.1 9.3 %collective-permute-start.26 = (f32[6,50,1]{2,1,0:T(8,128)S(1)}, f32[6,50,1]{2,1,0:T(8,128)S(1)}, u32[]{:S(2)}, u32[]{:S(2)}) collective-permute-start(f32[6,50,1]{2,1,0:T(8,128)S(1)} %get-tuple-element.30), channel_id=1, source_target_pairs={{1,0},{2,1},{3,2},{4,3},{5,4},{6,5},{7,6},{8,7},{9,8},{10,9},{11,1... | collective-permute-start | bytes 3608 | tf_op jit(solution)/shard_map/ppermute | solution.py:21
  161.5 10.1 %collective-permute-start.28 = (f32[6,1,128]{2,1,0:T(1,128)S(1)}, f32[6,1,128]{2,1,0:T(1,128)S(1)}, u32[]{:S(2)}, u32[]{:S(2)}) collective-permute-start(f32[6,1,128]{2,1,0:T(1,128)S(1)} %get-tuple-element.47), channel_id=1, source_target_pairs={{0,16},{16,32},{32,48},{48,64},{64,80},{80,96},{96,112},{112,128},... | collective-permute-start | bytes 9224 | tf_op jit(solution)/shard_map/ppermute | solution.py:19
  172.4 9.3 %collective-permute-start.30 = (f32[6,50,1]{2,1,0:T(8,128)S(1)}, f32[6,50,1]{2,1,0:T(8,128)S(1)}, u32[]{:S(2)}, u32[]{:S(2)}) collective-permute-start(f32[6,50,1]{2,1,0:T(8,128)S(1)} %get-tuple-element.28), channel_id=1, source_target_pairs={{1,0},{2,1},{3,2},{4,3},{5,4},{6,5},{7,6},{8,7},{9,8},{10,9},{11,1... | collective-permute-start | bytes 3608 | tf_op jit(solution)/shard_map/ppermute | solution.py:21
  184.7 10.1 %collective-permute-start.32 = (f32[6,1,128]{2,1,0:T(1,128)S(1)}, f32[6,1,128]{2,1,0:T(1,128)S(1)}, u32[]{:S(2)}, u32[]{:S(2)}) collective-permute-start(f32[6,1,128]{2,1,0:T(1,128)S(1)} %get-tuple-element.45), channel_id=1, source_target_pairs={{0,16},{16,32},{32,48},{48,64},{64,80},{80,96},{96,112},{112,128},... | collective-permute-start | bytes 9224 | tf_op jit(solution)/shard_map/ppermute | solution.py:19
  195.6 9.3 %collective-permute-start.34 = (f32[6,50,1]{2,1,0:T(8,128)S(1)}, f32[6,50,1]{2,1,0:T(8,128)S(1)}, u32[]{:S(2)}, u32[]{:S(2)}) collective-permute-start(f32[6,50,1]{2,1,0:T(8,128)S(1)} %get-tuple-element.26), channel_id=1, source_target_pairs={{1,0},{2,1},{3,2},{4,3},{5,4},{6,5},{7,6},{8,7},{9,8},{10,9},{11,1... | collective-permute-start | bytes 3608 | tf_op jit(solution)/shard_map/ppermute | solution.py:21
  209.3 10.1 %collective-permute-start.36 = (f32[6,1,128]{2,1,0:T(1,128)S(1)}, f32[6,1,128]{2,1,0:T(1,128)S(1)}, u32[]{:S(2)}, u32[]{:S(2)}) collective-permute-start(f32[6,1,128]{2,1,0:T(1,128)S(1)} %get-tuple-element.41), channel_id=1, source_target_pairs={{0,16},{16,32},{32,48},{48,64},{64,80},{80,96},{96,112},{112,128},... | collective-permute-start | bytes 9224 | tf_op jit(solution)/shard_map/ppermute | solution.py:19
  220.2 9.3 %collective-permute-start.38 = (f32[6,50,1]{2,1,0:T(8,128)S(1)}, f32[6,50,1]{2,1,0:T(8,128)S(1)}, u32[]{:S(2)}, u32[]{:S(2)}) collective-permute-start(f32[6,50,1]{2,1,0:T(8,128)S(1)} %get-tuple-element.24), channel_id=1, source_target_pairs={{1,0},{2,1},{3,2},{4,3},{5,4},{6,5},{7,6},{8,7},{9,8},{10,9},{11,1... | collective-permute-start | bytes 3608 | tf_op jit(solution)/shard_map/ppermute | solution.py:21
  (21 other events, 151.8 us)
where the time goes:
time: 237 us; the launch traced here: 233 us
  starting transfers between devices  196 us (83%)
  waiting for transfers between devices  23.2 us (10%)
  other arithmetic  9.83 us (4%)
  local copies, waits for them, and re-layouts  2.37 us (1%)
    ppermute x20, starting transfers between devices, padded_2(): lax.ppermute(head, axis, [((i + 1) % count, i) for i in range(count)])  150 us
    ppermute x20, starting transfers between devices, padded_2(): lax.ppermute(tail, axis, [(i, (i + 1) % count) for i in range(count)])  46.1 us
    ppermute x20, waiting for transfers between devices, padded_2(): lax.ppermute(tail, axis, [(i, (i + 1) % count) for i in range(count)])  18.2 us
    ppermute x20, waiting for transfers between devices, padded_2(): lax.ppermute(head, axis, [((i + 1) % count, i) for i in range(count)])  5.02 us
  transfers between devices with their start and end apart: 40, of which 15 were waited for; matrix products, arithmetic and copies ran while one was open for 1% of the time, Pallas kernels for 0%

commit v1 on v0

v1 whole, which is shorter than its diff:
```python
import jax
import jax.numpy as jnp
from jax import lax
from jax.experimental import pallas as pl
from jax.experimental.pallas import tpu as pltpu
from jax.sharding import PartitionSpec as P

MESH = pl.DeviceIdType.MESH
STEPS = 4
K = 6
ROWS = 48
LANES = 128
TILES = 8
PAD = 80
VERTICAL = 0.04
F32 = jnp.float32

STATE, WET, SOURCE, COEF, COT = 0, 6, 12, 18, 20
PLANES = 26
PAIRS = PLANES // 2


def lane_roll(x, shift):
    return pltpu.roll(x, shift % LANES, x.ndim - 1)


def kernel(
    state_hbm, source_hbm, cot_hbm, coef_hbm, mask_hbm, bottom_hbm,
    final_ref, gini_ref, gsrc_ref,
    u_a, u_b, wet, src, cot, coef, mask, bottom,
    c_e, c_w, c_n, c_z, diag, gain,
    packed, pack_e, pack_w, corner_out, got_w, got_e, corner_in,
    s_a, s_b, s_c, s_src, s_cot, s_gain,
    load_sem, send_sem, recv_sem,
):
    lat, lon = lax.axis_index("lat"), lax.axis_index("lon")
    n_lat, n_lon = lax.axis_size("lat"), lax.axis_size("lon")
    up, down = lax.rem(lat + 1, n_lat), lax.rem(lat + n_lat - 1, n_lat)
    east, west = lax.rem(lon + 1, n_lon), lax.rem(lon + n_lon - 1, n_lon)
    neighbours = [
        (up, lon), (down, lon), (lat, east), (lat, west),
        (up, east), (up, west), (down, east), (down, west),
    ]

    lane = lax.broadcasted_iota(jnp.int32, (1, 8, LANES), 2)
    sub = lax.broadcasted_iota(jnp.int32, (1, 8, LANES), 1)
    block = lane // 16
    left = lane % 16 < 8
    own = pl.ds(16, ROWS)

    loads = [
        pltpu.make_async_copy(src_ref, dst_ref, load_sem.at[i])
        for i, (src_ref, dst_ref) in enumerate(
            [
                (bottom_hbm, bottom),
                (mask_hbm, mask),
                (coef_hbm, coef.at[:, own]),
                (state_hbm, u_a.at[:, own]),
                (source_hbm, src.at[:, own]),
                (cot_hbm, cot.at[:, own]),
            ]
        )
    ]
    for load in loads:
        load.start()

    zero_tile = jnp.zeros((K, 8, LANES), F32)
    for ref in (u_a, u_b, wet):
        ref[:, 0:8] = zero_tile
        ref[:, 72:80] = zero_tile
    coef[:, 0:8] = zero_tile[:2]
    coef[:, 72:80] = zero_tile[:2]
    c_n[:, 0:8] = zero_tile
    packed[:, :, :] = jnp.zeros((PLANES, 8, LANES), F32)

    barrier = pltpu.get_barrier_semaphore()
    for device in neighbours:
        pl.semaphore_signal(barrier, inc=1, device_id=device, device_id_type=MESH)

    def pack_own(values, plane, count):
        for k in range(count):
            total = packed[plane + k : plane + k + 1]
            for j in range(6):
                moved = lane_roll(values(k, j), 16 * (j + 1) + 8)
                total = jnp.where(block == j + 1, moved, total)
            packed[plane + k : plane + k + 1] = total

    loads[0].wait()
    loads[1].wait()
    for k in range(K):
        wet[k, 16 : 16 + ROWS] = jnp.where(k < bottom[...], mask[k], 0).astype(F32)
    loads[2].wait()
    closed = jnp.logical_and(sub == 7, lat == n_lat - 1)
    coef[1:2, 56:64] = jnp.where(closed, 0.0, coef[1:2, 56:64])

    def tile_of(ref):
        return lambda k, j: ref[k : k + 1, 16 + 8 * j : 24 + 8 * j]

    pack_own(tile_of(wet), WET, K)
    pack_own(tile_of(coef), COEF, 2)
    loads[3].wait()
    pack_own(tile_of(u_a), STATE, K)
    loads[4].wait()
    pack_own(tile_of(src), SOURCE, K)
    loads[5].wait()
    pack_own(tile_of(cot), COT, K)

    for i in range(PAIRS):
        first, second = packed[2 * i : 2 * i + 1], packed[2 * i + 1 : 2 * i + 2]
        pack_e[i : i + 1] = jnp.where(left, first, lane_roll(second, 8))
        pack_w[i : i + 1] = jnp.where(left, lane_roll(first, -8), second)
    for c, (ref, source_block) in enumerate(((pack_e, 6), (pack_w, 6), (pack_e, 1), (pack_w, 1))):
        for v in range(2):
            total = jnp.zeros((1, 8, LANES), F32)
            for j in range(min(8, PAIRS - 8 * v)):
                i = 8 * v + j
                moved = lane_roll(ref[i : i + 1], 16 * (j - source_block))
                total = jnp.where(block == j, moved, total)
            corner_out[c, v : v + 1] = total

    pl.semaphore_wait(barrier, len(neighbours))

    copies = []

    def send(src_ref, dst_ref, device):
        i = len(copies)
        copy = pltpu.make_async_remote_copy(
            src_ref=src_ref, dst_ref=dst_ref, send_sem=send_sem.at[i], recv_sem=recv_sem.at[i],
            device_id=device, device_id_type=MESH,
        )
        copy.start()
        copies.append(copy)
        return copy

    top, bot = pl.ds(56, 8), pl.ds(16, 8)
    low, high = pl.ds(8, 8), pl.ds(64, 8)
    corners = [
        send(corner_out.at[c], corner_in.at[c], device)
        for c, device in enumerate(((up, east), (up, west), (down, east), (down, west)))
    ]
    strips = [send(pack_e, got_w, (lat, east)), send(pack_w, got_e, (lat, west))]
    rows = {}
    for name, ref in (("wet", wet), ("coef", coef), ("state", u_a), ("src", src), ("cot", cot)):
        rows[name] = [
            send(ref.at[:, top], ref.at[:, low], (up, lon)),
            send(ref.at[:, bot], ref.at[:, high], (down, lon)),
        ]

    for copy in corners + strips:
        copy.wait_recv()
    for ref, low_corner, high_corner in ((got_w, 0, 2), (got_e, 1, 3)):
        for i in range(PAIRS):
            v, j = i // 8, i % 8
            total = ref[i : i + 1]
            total = jnp.where(block == 0, lane_roll(corner_in[low_corner, v : v + 1], -16 * j), total)
            total = jnp.where(block == 7, lane_roll(corner_in[high_corner, v : v + 1], 16 * (7 - j)), total)
            ref[i : i + 1] = total

    for name in rows:
        for copy in rows[name]:
            copy.wait_recv()
    for copy in copies:
        copy.wait_send()

    for plane, ref, count in ((STATE, u_a, K), (WET, wet, K), (SOURCE, src, K), (COEF, coef, 2), (COT, cot, K)):
        for k in range(count):
            total = packed[plane + k : plane + k + 1]
            total = jnp.where(block == 0, lane_roll(ref[k : k + 1, 8:16], 8), total)
            total = jnp.where(block == 7, lane_roll(ref[k : k + 1, 64:72], 120), total)
            packed[plane + k : plane + k + 1] = total

    def strip(plane):
        i = plane // 2
        mine, from_west, from_east = packed[plane : plane + 1], got_w[i : i + 1], got_e[i : i + 1]
        if plane % 2 == 0:
            return jnp.where(left, from_west, mine), jnp.where(left, mine, lane_roll(from_east, 8))
        return jnp.where(left, lane_roll(from_west, -8), mine), jnp.where(left, mine, from_east)

    def strips_of(plane, count):
        return jnp.concatenate([part for k in range(count) for part in strip(plane + k)], 0)

    def s_north(x):
        rolled = pltpu.roll(x, 7, 1)
        return jnp.where(sub == 7, lane_roll(rolled, -16), rolled)

    def s_south(x):
        rolled = pltpu.roll(x, 1, 1)
        return jnp.where(sub == 0, lane_roll(rolled, 16), rolled)

    def joined(x):
        return [jnp.where(left, x[2 * k : 2 * k + 1], x[2 * k + 1 : 2 * k + 2]) for k in range(x.shape[0] // 2)]

    def beside(x, outer, r):
        turned = lane_roll(outer, 120 - 16 * r)
        return (
            lane_roll(jnp.where(lane == 0, turned, x), -1),
            lane_roll(jnp.where(lane == LANES - 1, turned, x), 1),
        )

    def six(x, y):
        return jnp.concatenate([x, y] * K, 0)

    w = strips_of(WET, K)
    coef_e, coef_n = strips_of(COEF, 2)[0:2], strips_of(COEF, 2)[2:4]
    all_e, all_n = six(coef_e[0:1], coef_e[1:2]), six(coef_n[0:1], coef_n[1:2])
    s_ce = all_e * w * lane_roll(w, -1)
    s_cw = lane_roll(all_e, 1) * lane_roll(w, 1) * w
    s_cn = all_n * w * s_north(w)
    s_cs = s_south(all_n) * s_south(w) * w
    s_cz = VERTICAL * (w[:-2] * w[2:])
    nothing = jnp.zeros((2, 8, LANES), F32)
    s_d = 1.0 - (s_ce + s_cw) - (s_cn + s_cs)
    s_d = s_d - jnp.concatenate([s_cz, nothing], 0) - jnp.concatenate([nothing, s_cz], 0)
    for i, part in enumerate((s_d, s_ce, s_cw, s_cn, s_cs)):
        s_c[i] = part
    s_c[5, 0:10] = s_cz
    s_src[...] = strips_of(SOURCE, K)
    s_cot[...] = strips_of(COT, K)
    s_a[...] = strips_of(STATE, K)
    wet_outer = joined(w)
    coef_outer = joined(coef_e)[0]

    for r in range(TILES):
        at = 8 + 8 * r
        ce, cn, cs = coef[0:1, at : at + 8], coef[1:2, at : at + 8], coef[1:2, at - 1 : at + 7]
        _, ce_west = beside(ce, coef_outer, r)
        tiles = [wet[k : k + 1, at : at + 8] for k in range(K)]
        below = None
        for k in range(K):
            wk = tiles[k]
            w_east, w_west = beside(wk, wet_outer[k], r)
            e, wst = ce * wk * w_east, ce_west * w_west * wk
            n = cn * wk * wet[k : k + 1, at + 1 : at + 9]
            s = cs * wet[k : k + 1, at - 1 : at + 7] * wk
            d = 1.0 - (e + wst) - (n + s)
            if k < K - 1:
                z = VERTICAL * (wk * tiles[k + 1])
                c_z[k : k + 1, 8 * r : 8 * r + 8] = z
                d = d - z
            if below is not None:
                d = d - below
            below = z
            c_e[k : k + 1, 8 * r : 8 * r + 8] = e
            c_w[k : k + 1, 8 * r : 8 * r + 8] = wst
            c_n[k : k + 1, at : at + 8] = n
            diag[k : k + 1, 8 * r : 8 * r + 8] = d

    def strip_product(ref):
        x = ref[...]
        out = s_c[0] * x + (s_c[1] * lane_roll(x, -1) + s_c[2] * lane_roll(x, 1))
        out = out + (s_c[3] * s_north(x) + s_c[4] * s_south(x))
        cz = s_c[5, 0:10]
        out = out + jnp.concatenate([cz * x[2:], nothing], 0) + jnp.concatenate([nothing, cz * x[:-2]], 0)
        return out, joined(x)

    def product(ref, outer, r):
        at, t = 8 + 8 * r, 8 * r
        x = [ref[k : k + 1, at : at + 8] for k in range(K)]
        out = []
        for k in range(K):
            x_east, x_west = beside(x[k], outer[k], r)
            p = diag[k : k + 1, t : t + 8] * x[k]
            p = p + (c_e[k : k + 1, t : t + 8] * x_east + c_w[k : k + 1, t : t + 8] * x_west)
            p = p + (
                c_n[k : k + 1, at : at + 8] * ref[k : k + 1, at + 1 : at + 9]
                + c_n[k : k + 1, at - 1 : at + 7] * ref[k : k + 1, at - 1 : at + 7]
            )
            if k < K - 1:
                p = p + c_z[k : k + 1, t : t + 8] * x[k + 1]
            if k > 0:
                p = p + c_z[k - 1 : k, t : t + 8] * x[k - 1]
            out.append(p)
        return out

    def forward(n, now, later, s_now, s_later):
        p, outer = strip_product(s_now)
        bounded = jnp.tanh(p)
        s_gain[n] = 1.0 - bounded * bounded
        s_later[...] = bounded + s_src[...]
        for r in range(TILES):
            at = 8 + 8 * r
            for k, p in enumerate(product(now, outer, r)):
                bounded = jnp.tanh(p)
                gain[n, k : k + 1, 8 * r : 8 * r + 8] = 1.0 - bounded * bounded
                later[k : k + 1, at : at + 8] = bounded + src[k : k + 1, at : at + 8]

    def forward_two(i, carry):
        forward(2 * i, u_a, u_b, s_a, s_b)
        forward(2 * i + 1, u_b, u_a, s_b, s_a)
        return carry

    lax.fori_loop(0, STEPS // 2, forward_two, 0)

    for r in range(TILES):
        at = 8 + 8 * r
        for k in range(K):
            if 1 <= r <= 6:
                o = 8 * r - 8
                final_ref[k : k + 1, o : o + 8] = wet[k : k + 1, at : at + 8] * u_a[k : k + 1, at : at + 8]
                gsrc_ref[k : k + 1, o : o + 8] = cot[k : k + 1, at : at + 8]
            u_a[k : k + 1, at : at + 8] = gain[STEPS - 1, k : k + 1, 8 * r : 8 * r + 8] * cot[k : k + 1, at : at + 8]
    s_a[...] = s_gain[STEPS - 1] * s_cot[...]

    def backward(n, now, later, s_now, s_later):
        p, outer = strip_product(s_now)
        s_later[...] = s_gain[n - 1] * p
        for r in range(TILES):
            at = 8 + 8 * r
            for k, p in enumerate(product(now, outer, r)):
                later[k : k + 1, at : at + 8] = gain[n - 1, k : k + 1, 8 * r : 8 * r + 8] * p
                if 1 <= r <= 6:
                    o = 8 * r - 8
                    gsrc_ref[k : k + 1, o : o + 8] += p

    backward(3, u_a, u_b, s_a, s_b)
    backward(2, u_b, u_a, s_b, s_a)
    backward(1, u_a, u_b, s_a, s_b)
    outer = joined(s_b[...])
    for r in range(1, 7):
        at, o = 8 + 8 * r, 8 * r - 8
        for k, p in enumerate(product(u_b, outer, r)):
            w = wet[k : k + 1, at : at + 8]
            gini_ref[k : k + 1, o : o + 8] = w * p
            gsrc_ref[k : k + 1, o : o + 8] = w * gsrc_ref[k : k + 1, o : o + 8]


def body(initial_state, source, cotangent, face_coefs, land_mask, bottom):
    out = jax.ShapeDtypeStruct((K, ROWS, LANES), F32)
    rows = pltpu.VMEM((K, PAD, LANES), F32)
    tiles = pltpu.VMEM((K, 8 * TILES, LANES), F32)
    strips = pltpu.VMEM((2 * K, 8, LANES), F32)
    pairs = pltpu.VMEM((PAIRS, 8, LANES), F32)
    return pl.pallas_call(
        kernel,
        name="window",
        out_shape=(out, out, out),
        in_specs=[pl.BlockSpec(memory_space=pl.ANY)] * 6,
        out_specs=(pl.BlockSpec(memory_space=pltpu.VMEM),) * 3,
        scratch_shapes=[
            rows, rows, rows, rows, rows,
            pltpu.VMEM((2, PAD, LANES), F32),
            pltpu.VMEM((K, ROWS, LANES), jnp.int32),
            pltpu.VMEM((ROWS, LANES), jnp.int32),
            tiles, tiles, rows, tiles, tiles,
            pltpu.VMEM((STEPS, K, 8 * TILES, LANES), F32),
            pltpu.VMEM((PLANES, 8, LANES), F32),
            pairs, pairs,
            pltpu.VMEM((4, 2, 8, LANES), F32),
            pairs, pairs,
            pltpu.VMEM((4, 2, 8, LANES), F32),
            strips, strips,
            pltpu.VMEM((6, 2 * K, 8, LANES), F32),
            strips, strips,
            pltpu.VMEM((STEPS, 2 * K, 8, LANES), F32),
            pltpu.SemaphoreType.DMA((6,)),
            pltpu.SemaphoreType.DMA((16,)),
            pltpu.SemaphoreType.DMA((16,)),
        ],
        compiler_params=pltpu.CompilerParams(collective_id=0, has_side_effects=True),
    )(initial_state, source, cotangent, face_coefs, land_mask, bottom)


def solution(mesh):
    spec = P(None, "lat", "lon")
    return jax.shard_map(
        body,
        mesh=mesh,
        in_specs=(spec,) * 5 + (P("lat", "lon"),),
        out_specs=(spec,) * 3,
        check_vma=False,
    )
```

time: 237 us -> 53.7 us (0.23); the launches traced: 233 us -> 53.5 us
  starting transfers between devices: 196 us -> 0 us
  Pallas kernels: 0 us -> 49.6 us
  waiting for transfers between devices: 23.2 us -> 0 us
  other arithmetic: 9.83 us -> 0 us
    ppermute x40 -> x0, starting transfers between devices: 196 us -> none  [the longest x20 150 us: padded_2(): lax.ppermute(head, axis, [((i + 1) % count, i) for i in range(count)])]
    pallas_call x0 -> x1, Pallas kernels: none -> 49.6 us  [body(): pl.pallas_call(kernel, name='window', out_shape=(out, out, out), in_specs...]
    ppermute x40 -> x0, waiting for transfers between devices: 23.2 us -> none  [the longest x20 18.2 us: padded_2(): lax.ppermute(tail, axis, [(i, (i + 1) % count) for i in range(count)])]
    mul x31 -> x0, other arithmetic: 4.13 us -> none  [the longest x8 1.61 us: operate(): coef_lon[None, :, :-1] * (wet_mask[:, :, :-1] * wet_mask[:, :, 1:])]
  transfers between devices with their start and end apart: 40 -> 0, of which waited for: 15 -> 0; matrix products, arithmetic and copies ran while one was open for 1% -> 0% of each run, Pallas kernels for 0% -> 0%
where the time goes in v1:
time: 53.7 us; the launch traced here: 53.5 us
  Pallas kernels  49.6 us (92%)
  local copies, waits for them, and re-layouts  3.25 us (6%)
  between operations  0.65 us (1%)
    pallas_call x1, Pallas kernels, body(): pl.pallas_call(kernel, name='window', out_shape=(out, out, out), in_specs...  49.6 us
    unnamed x7, local copies, waits for them, and re-layouts  3.25 us

profile of v1, /device:TPU:1, one launch (start us, length us, event | category | flops | bytes accessed | tf_op | source)
XLA Modules:
  0.0 53.5 jit_solution(5757307438659213891)
XLA Ops:
  0.6 49.6 %window.1 = (f32[6,48,128]{2,1,0:T(8,128)}, f32[6,48,128]{2,1,0:T(8,128)}, f32[6,48,128]{2,1,0:T(8,128)}) custom-call(f32[6,48,128]{2,1,0:T(8,128)} %state_hbm.1, f32[6,48,128]{2,1,0:T(8,128)} %source_hbm.1, f32[6,48,128]{2,1,0:T(8,128)} %cot_hbm.1, f32[2,48,128]{2,1,0:T(8,128)} %coef_hbm.1, s32[6,48,128]{2,1,0:T(8,128)} %mask_hbm.1, s32[48,128]{1,0:T(8,128)} %bottom_hbm.1), custom_call_target="tpu_custom_call" | custom-call | tf_op jit(solution)/shard_map/window/pallas_call | solution.py:333
  50.2 0.0 copy-start.1
  50.2 1.6 %copy.12 = f32[6,48,128]{2,1,0:T(8,128)} copy(f32[6,48,128]{2,1,0:T(8,128)} %get-tuple-element.6) | data formatting | bytes 294912
  51.8 0.0 copy-done.1
  51.8 0.0 copy-start
  51.8 0.7 %copy.13 = f32[6,48,128]{2,1,0:T(8,128)} copy(f32[6,48,128]{2,1,0:T(8,128)S(1)} %copy-done.1) | data formatting | bytes 294912
  52.5 0.3 copy-done
  52.8 0.7 %copy.14 = f32[6,48,128]{2,1,0:T(8,128)} copy(f32[6,48,128]{2,1,0:T(8,128)S(1)} %copy-done) | data formatting | bytes 294912
Async XLA Ops:
  50.2 1.6 %copy-start.1 = (f32[6,48,128]{2,1,0:T(8,128)S(1)}, f32[6,48,128]{2,1,0:T(8,128)}, u32[]{:S(2)}) copy-start(f32[6,48,128]{2,1,0:T(8,128)} %get-tuple-element.7) | copy-start | bytes 442372
  51.8 1.0 %copy-start = (f32[6,48,128]{2,1,0:T(8,128)S(1)}, f32[6,48,128]{2,1,0:T(8,128)}, u32[]{:S(2)}) copy-start(f32[6,48,128]{2,1,0:T(8,128)} %get-tuple-element.8) | copy-start | bytes 442372

commit v2 on v0

v2 whole, which is shorter than its diff:
```python
import jax
import jax.numpy as jnp
from jax import lax
from jax.experimental import pallas as pl
from jax.experimental.pallas import tpu as pltpu
from jax.sharding import PartitionSpec as P

MESH = pl.DeviceIdType.MESH
STEPS = 4
K = 6
ROWS = 48
LANES = 128
TILES = 8
PAD = 80
UNROLL = 8
PAIR_UNROLL = 7
COEF_UNROLL = 2
VERTICAL = 0.04
F32 = jnp.float32

STATE, WET, SOURCE, COEF, COT, OTHER = 0, 6, 12, 18, 20, 26
PLANES = 26
PAIRS = PLANES // 2 + 1


def lane_roll(x, shift):
    if isinstance(shift, int):
        shift %= LANES
    return pltpu.roll(x, shift, x.ndim - 1)


def kernel(
    state_hbm, source_hbm, cot_hbm, coef_hbm, mask_hbm, bottom_hbm,
    final_ref, gini_ref, gsrc_ref,
    x_ref, mask, bottom,
    c_e, c_w, c_n, c_z, diag, gain, adj,
    packed, pack_e, pack_w, corner_out, got_w, got_e, corner_in,
    s_ref, s_c, s_gain,
    load_sem, send_sem, recv_sem,
):
    lat, lon = lax.axis_index("lat"), lax.axis_index("lon")
    n_lat, n_lon = lax.axis_size("lat"), lax.axis_size("lon")
    up, down = lax.rem(lat + 1, n_lat), lax.rem(lat + n_lat - 1, n_lat)
    east, west = lax.rem(lon + 1, n_lon), lax.rem(lon + n_lon - 1, n_lon)
    neighbours = [
        (up, lon), (down, lon), (lat, east), (lat, west),
        (up, east), (up, west), (down, east), (down, west),
    ]

    barrier = pltpu.get_barrier_semaphore()
    for device in neighbours:
        pl.semaphore_signal(barrier, inc=1, device_id=device, device_id_type=MESH)

    lane = lax.broadcasted_iota(jnp.int32, (1, 8, LANES), 2)
    sub = lax.broadcasted_iota(jnp.int32, (1, 8, LANES), 1)
    block = lane // 16
    left = lane % 16 < 8
    own = pl.ds(16, ROWS)

    def planes(start, count):
        return x_ref.at[pl.ds(start, count)]

    fields = [
        (mask_hbm, mask, 8),
        (bottom_hbm, bottom, 8),
        (coef_hbm, planes(COEF, 2), 16),
        (state_hbm, planes(STATE, K), 16),
        (source_hbm, planes(SOURCE, K), 16),
        (cot_hbm, planes(COT, K), 16),
    ]

    def rows_of(ref, start, size):
        if len(ref.shape) == 2:
            return ref.at[pl.ds(start, size)]
        return ref.at[:, pl.ds(start, size)]

    loads = [
        pltpu.make_async_copy(hbm, rows_of(ref, first, ROWS), load_sem.at[i])
        for i, (hbm, ref, first) in enumerate(fields)
    ]
    for load in loads:
        load.start()

    zero_tile = jnp.zeros((1, 8, LANES), F32)

    def clear(p, carry):
        x_ref[pl.ds(p, 1), 0:8] = zero_tile
        x_ref[pl.ds(p, 1), 72:80] = zero_tile
        return carry

    lax.fori_loop(0, PLANES + K, clear, 0)
    c_n[:, 0:8] = jnp.zeros((K, 8, LANES), F32)

    pl.semaphore_wait(barrier, len(neighbours))

    copies = []

    def send(src_ref, dst_ref, device):
        i = len(copies)
        copy = pltpu.make_async_remote_copy(
            src_ref=src_ref, dst_ref=dst_ref, send_sem=send_sem.at[i], recv_sem=recv_sem.at[i],
            device_id=device, device_id_type=MESH,
        )
        copy.start()
        copies.append(copy)
        return copy

    rows = []
    for hbm, ref, first in fields:
        rows.append(send(rows_of(hbm, ROWS - 8, 8), rows_of(ref, first - 8, 8), (up, lon)))
        rows.append(send(rows_of(hbm, 0, 8), rows_of(ref, first + ROWS, 8), (down, lon)))

    def wet_rows(start, size):
        for k in range(K):
            here = pl.ds(start, size)
            x_ref[WET + k, pl.ds(start + 8, size)] = jnp.where(k < bottom[here], mask[k, here], 0).astype(F32)

    def close(at, condition):
        tile = x_ref[COEF + 1 : COEF + 2, at : at + 8]
        x_ref[COEF + 1 : COEF + 2, at : at + 8] = jnp.where(jnp.logical_and(sub == 7, condition), 0.0, tile)

    for load in loads:
        load.wait()
    wet_rows(8, ROWS)
    close(56, lat == n_lat - 1)

    def by_pair(one):
        def several(i, carry):
            for q in range(PAIR_UNROLL):
                one(i * PAIR_UNROLL + q)
            return carry

        lax.fori_loop(0, PAIRS // PAIR_UNROLL, several, 0)

    def pack(i):
        both = []
        for q in range(2):
            total = zero_tile
            for j in range(6):
                moved = lane_roll(x_ref[pl.ds(2 * i + q, 1), 16 + 8 * j : 24 + 8 * j], 16 * (j + 1) + 8)
                total = moved if j == 0 else jnp.where(block == j + 1, moved, total)
            packed[pl.ds(2 * i + q, 1)] = total
            both.append(total)
        to_east = jnp.where(left, both[0], lane_roll(both[1], 8))
        to_west = jnp.where(left, lane_roll(both[0], -8), both[1])
        pack_e[pl.ds(i, 1)] = to_east
        pack_w[pl.ds(i, 1)] = to_west
        v, j = i // 8, i % 8
        for c, (value, source_block) in enumerate(((to_east, 6), (to_west, 6), (to_east, 1), (to_west, 1))):
            moved = lane_roll(value, lax.rem(16 * (j + 8 - source_block), LANES))
            corner_out[c, pl.ds(v, 1)] = jnp.where(block == j, moved, corner_out[c, pl.ds(v, 1)])

    by_pair(pack)

    corners = [
        send(corner_out.at[c], corner_in.at[c], device)
        for c, device in enumerate(((up, east), (up, west), (down, east), (down, west)))
    ]
    strips = [send(pack_e, got_w, (lat, east)), send(pack_w, got_e, (lat, west))]

    for copy in rows:
        copy.wait_recv()
    wet_rows(0, 8)
    wet_rows(ROWS + 8, 8)
    close(8, lat == 0)
    for copy in corners + strips:
        copy.wait_recv()

    def unpack(i):
        v, j = i // 8, i % 8
        sides = []
        for ref, low, high in ((got_w, 0, 2), (got_e, 1, 3)):
            total = ref[pl.ds(i, 1)]
            total = jnp.where(block == 0, lane_roll(corner_in[low, pl.ds(v, 1)], lax.rem(LANES - 16 * j, LANES)), total)
            total = jnp.where(block == 7, lane_roll(corner_in[high, pl.ds(v, 1)], 16 * (7 - j)), total)
            sides.append(total)
        from_west, from_east = sides
        for q in range(2):
            p = 2 * i + q
            mine = packed[pl.ds(p, 1)]
            mine = jnp.where(block == 0, lane_roll(x_ref[pl.ds(p, 1), 8:16], 8), mine)
            mine = jnp.where(block == 7, lane_roll(x_ref[pl.ds(p, 1), 64:72], 120), mine)
            a = from_west if q == 0 else lane_roll(from_west, -8)
            b = lane_roll(from_east, 8) if q == 0 else from_east
            s_ref[pl.ds(2 * p, 1)] = jnp.where(left, a, mine)
            s_ref[pl.ds(2 * p + 1, 1)] = jnp.where(left, mine, b)

    by_pair(unpack)

    def s_north(x):
        rolled = pltpu.roll(x, 7, 1)
        return jnp.where(sub == 7, lane_roll(rolled, -16), rolled)

    def s_south(x):
        rolled = pltpu.roll(x, 1, 1)
        return jnp.where(sub == 0, lane_roll(rolled, 16), rolled)

    def beside(x, a, b, r):
        turned = lane_roll(jnp.where(left, a, b), lax.rem(120 + LANES - 16 * r, LANES))
        return (
            lane_roll(jnp.where(lane == 0, turned, x), -1),
            lane_roll(jnp.where(lane == LANES - 1, turned, x), 1),
        )

    def level(p):
        return s_ref[2 * p : 2 * p + 1], s_ref[2 * p + 1 : 2 * p + 2]

    def six(pair):
        return jnp.concatenate([pair] * K, 0)

    w = s_ref[2 * WET : 2 * WET + 2 * K]
    all_e = six(s_ref[2 * COEF : 2 * COEF + 2])
    all_n = six(s_ref[2 * COEF + 2 : 2 * COEF + 4])
    s_ce = all_e * w * lane_roll(w, -1)
    s_cw = lane_roll(all_e, 1) * lane_roll(w, 1) * w
    s_cn = all_n * w * s_north(w)
    s_cs = s_south(all_n) * s_south(w) * w
    s_cz = VERTICAL * (w[:-2] * w[2:])
    nothing = jnp.zeros((2, 8, LANES), F32)
    s_d = 1.0 - (s_ce + s_cw) - (s_cn + s_cs)
    s_d = s_d - jnp.concatenate([s_cz, nothing], 0) - jnp.concatenate([nothing, s_cz], 0)
    for i, part in enumerate((s_d, s_ce, s_cw, s_cn, s_cs)):
        s_c[i] = part
    s_c[5, 0:10] = s_cz

    def by_tile(count, unroll, one):
        def several(i, carry):
            for q in range(unroll):
                r = i * unroll + q
                t = pl.multiple_of(8 * r, 8)
                one(r, t)
            return carry

        lax.fori_loop(0, count // unroll, several, 0)

    def coefficients(r, t):
        at = pl.ds(t + 8, 8)
        ce, cn = x_ref[COEF : COEF + 1, at], x_ref[COEF + 1 : COEF + 2, at]
        cs = x_ref[COEF + 1 : COEF + 2, pl.ds(t + 7, 8)]
        _, ce_west = beside(ce, *level(COEF), r)
        tiles = [x_ref[WET + k : WET + k + 1, at] for k in range(K)]
        below = None
        for k in range(K):
            wk = tiles[k]
            w_east, w_west = beside(wk, *level(WET + k), r)
            e, wst = ce * wk * w_east, ce_west * w_west * wk
            n = cn * wk * x_ref[WET + k : WET + k + 1, pl.ds(t + 9, 8)]
            s = cs * x_ref[WET + k : WET + k + 1, pl.ds(t + 7, 8)] * wk
            d = 1.0 - (e + wst) - (n + s)
            if k < K - 1:
                z = VERTICAL * (wk * tiles[k + 1])
                c_z[k : k + 1, pl.ds(t, 8)] = z
                d = d - z
            if below is not None:
                d = d - below
            below = z
            c_e[k : k + 1, pl.ds(t, 8)] = e
            c_w[k : k + 1, pl.ds(t, 8)] = wst
            c_n[k : k + 1, at] = n
            diag[k : k + 1, pl.ds(t, 8)] = d

    by_tile(TILES, COEF_UNROLL, coefficients)

    def strip_product(base):
        x = s_ref[pl.ds(2 * base, 2 * K)]
        out = s_c[0] * x + (s_c[1] * lane_roll(x, -1) + s_c[2] * lane_roll(x, 1))
        out = out + (s_c[3] * s_north(x) + s_c[4] * s_south(x))
        cz = s_c[5, 0:10]
        return out + jnp.concatenate([cz * x[2:], nothing], 0) + jnp.concatenate([nothing, cz * x[:-2]], 0)

    def product(base, r, t):
        here, at = pl.ds(t, 8), pl.ds(t + 8, 8)
        north, south = pl.ds(t + 9, 8), pl.ds(t + 7, 8)
        x = [x_ref[pl.ds(base + k, 1), at] for k in range(K)]
        out = []
        for k in range(K):
            one = pl.ds(base + k, 1)
            x_east, x_west = beside(x[k], s_ref[pl.ds(2 * (base + k), 1)], s_ref[pl.ds(2 * (base + k) + 1, 1)], r)
            p = diag[k : k + 1, here] * x[k]
            p = p + (c_e[k : k + 1, here] * x_east + c_w[k : k + 1, here] * x_west)
            p = p + (c_n[k : k + 1, at] * x_ref[one, north] + c_n[k : k + 1, south] * x_ref[one, south])
            if k < K - 1:
                p = p + c_z[k : k + 1, here] * x[k + 1]
            if k > 0:
                p = p + c_z[k - 1 : k, here] * x[k - 1]
            out.append(p)
        return out

    def forward(n, carry):
        now = OTHER * lax.rem(n, 2)
        later = OTHER - now
        bounded = jnp.tanh(strip_product(now))
        s_gain[n] = 1.0 - bounded * bounded
        s_ref[pl.ds(2 * later, 2 * K)] = bounded + s_ref[2 * SOURCE : 2 * SOURCE + 2 * K]

        def one(r, t):
            for k, p in enumerate(product(now, r, t)):
                bounded = jnp.tanh(p)
                gain[n, k : k + 1, pl.ds(t, 8)] = 1.0 - bounded * bounded
                at = pl.ds(t + 8, 8)
                x_ref[pl.ds(later + k, 1), at] = bounded + x_ref[SOURCE + k : SOURCE + k + 1, at]

        by_tile(TILES, UNROLL, one)
        return carry

    lax.fori_loop(0, STEPS, forward, 0)

    def turn(k, carry):
        one, o = pl.ds(k, 1), pl.ds(16, ROWS)
        final_ref[one] = x_ref[pl.ds(WET + k, 1), o] * x_ref[pl.ds(STATE + k, 1), o]
        x_ref[one, 8:72] = gain[STEPS - 1, one] * x_ref[pl.ds(COT + k, 1), 8:72]
        return carry

    lax.fori_loop(0, K, turn, 0)
    s_ref[0 : 2 * K] = s_gain[STEPS - 1] * s_ref[2 * COT : 2 * COT + 2 * K]

    def backward(m, carry):
        n = STEPS - 1 - m
        before = jnp.maximum(n - 1, 0)
        now = OTHER * lax.rem(m, 2)
        later = OTHER - now
        s_ref[pl.ds(2 * later, 2 * K)] = s_gain[before] * strip_product(now)

        def one(r, t):
            for k, p in enumerate(product(now, r, t)):
                here = pl.ds(t, 8)
                adj[n, k : k + 1, here] = p
                x_ref[pl.ds(later + k, 1), pl.ds(t + 8, 8)] = gain[before, k : k + 1, here] * p

        by_tile(TILES, UNROLL, one)
        return carry

    lax.fori_loop(0, STEPS, backward, 0)

    def finish(k, carry):
        one, o = pl.ds(k, 1), pl.ds(8, ROWS)
        wk = x_ref[pl.ds(WET + k, 1), 16 : 16 + ROWS]
        gini_ref[one] = wk * adj[0, one, o]
        gsrc_ref[one] = wk * (
            x_ref[pl.ds(COT + k, 1), 16 : 16 + ROWS] + adj[1, one, o] + (adj[2, one, o] + adj[3, one, o])
        )
        return carry

    lax.fori_loop(0, K, finish, 0)
    for copy in copies:
        copy.wait_send()


def store(a_ref, b_ref, c_ref, a_out, b_out, c_out, sem):
    copies = [
        pltpu.make_async_copy(src_ref, dst_ref, sem.at[i])
        for i, (src_ref, dst_ref) in enumerate(((a_ref, a_out), (b_ref, b_out), (c_ref, c_out)))
    ]
    for copy in copies:
        copy.start()
    for copy in copies:
        copy.wait()


def body(initial_state, source, cotangent, face_coefs, land_mask, bottom):
    out = pltpu.VMEM((K, ROWS, LANES), F32)
    tiles = pltpu.VMEM((K, 8 * TILES, LANES), F32)
    pairs = pltpu.VMEM((PAIRS, 8, LANES), F32)
    steps = pltpu.VMEM((STEPS, K, 8 * TILES, LANES), F32)
    corner = pltpu.VMEM((4, 2, 8, LANES), F32)
    results = pl.pallas_call(
        kernel,
        name="window",
        out_shape=(out, out, out),
        in_specs=[pl.BlockSpec(memory_space=pl.ANY)] * 6,
        out_specs=(pl.BlockSpec(memory_space=pltpu.VMEM),) * 3,
        scratch_shapes=[
            pltpu.VMEM((PLANES + K, PAD, LANES), F32),
            pltpu.VMEM((K, 8 * TILES, LANES), jnp.int32),
            pltpu.VMEM((8 * TILES, LANES), jnp.int32),
            tiles, tiles, pltpu.VMEM((K, PAD, LANES), F32), tiles, tiles,
            steps, steps,
            pltpu.VMEM((2 * PAIRS, 8, LANES), F32),
            pairs, pairs, corner, pairs, pairs, corner,
            pltpu.VMEM((2 * (PLANES + K), 8, LANES), F32),
            pltpu.VMEM((6, 2 * K, 8, LANES), F32),
            pltpu.VMEM((STEPS, 2 * K, 8, LANES), F32),
            pltpu.SemaphoreType.DMA((6,)),
            pltpu.SemaphoreType.DMA((18,)),
            pltpu.SemaphoreType.DMA((18,)),
        ],
        compiler_params=pltpu.CompilerParams(collective_id=0, has_side_effects=True),
    )(initial_state, source, cotangent, face_coefs, land_mask, bottom)
    plain = jax.ShapeDtypeStruct((K, ROWS, LANES), F32)
    return pl.pallas_call(
        store,
        name="store",
        out_shape=(plain,) * 3,
        in_specs=[pl.BlockSpec(memory_space=pltpu.VMEM)] * 3,
        out_specs=(pl.BlockSpec(memory_space=pl.ANY),) * 3,
        scratch_shapes=[pltpu.SemaphoreType.DMA((3,))],
    )(*[pltpu.with_memory_space_constraint(x, pltpu.VMEM) for x in results])


def solution(mesh):
    spec = P(None, "lat", "lon")
    return jax.shard_map(
        body,
        mesh=mesh,
        in_specs=(spec,) * 5 + (P("lat", "lon"),),
        out_specs=(spec,) * 3,
        check_vma=False,
    )
```

time: 237 us -> 34.2 us (0.14); the launches traced: 233 us -> 34 us
  starting transfers between devices: 196 us -> 0 us
  Pallas kernels: 0 us -> 33.4 us
  waiting for transfers between devices: 23.2 us -> 0 us
  other arithmetic: 9.83 us -> 0 us
  local copies, waits for them, and re-layouts: 2.37 us -> 0 us
    ppermute x40 -> x0, starting transfers between devices: 196 us -> none  [the longest x20 150 us: padded_2(): lax.ppermute(head, axis, [((i + 1) % count, i) for i in range(count)])]
    pallas_call x0 -> x2, Pallas kernels: none -> 33.4 us  [the longest x1 32.6 us: body(): pl.pallas_call(kernel, name='window', out_shape=(out, out, out), in_specs...]
    ppermute x40 -> x0, waiting for transfers between devices: 23.2 us -> none  [the longest x20 18.2 us: padded_2(): lax.ppermute(tail, axis, [(i, (i + 1) % count) for i in range(count)])]
    mul x31 -> x0, other arithmetic: 4.13 us -> none  [the longest x8 1.61 us: operate(): coef_lon[None, :, :-1] * (wet_mask[:, :, :-1] * wet_mask[:, :, 1:])]
  transfers between devices with their start and end apart: 40 -> 0, of which waited for: 15 -> 0; matrix products, arithmetic and copies ran while one was open for 1% -> 0% of each run, Pallas kernels for 0% -> 0%
where the time goes in v2:
time: 34.2 us; the launch traced here: 34 us
  Pallas kernels  33.4 us (98%)
  between operations  0.64 us (2%)
    pallas_call x1, Pallas kernels, body(): pl.pallas_call(kernel, name='window', out_shape=(out, out, out), in_specs...  32.6 us
    pallas_call x1, Pallas kernels, body(): pl.pallas_call(store, name='store', out_shape=(plain,) * 3, in_specs=[pl....  0.79 us

profile of v2, /device:TPU:1, one launch (start us, length us, event | category | flops | bytes accessed | tf_op | source)
XLA Modules:
  0.0 34.0 jit_solution(11150297574021348148)
XLA Ops:
  0.6 32.6 %window.1 = (f32[6,48,128]{2,1,0:T(8,128)S(1)}, f32[6,48,128]{2,1,0:T(8,128)S(1)}, f32[6,48,128]{2,1,0:T(8,128)S(1)}) custom-call(f32[6,48,128]{2,1,0:T(8,128)} %state_hbm.1, f32[6,48,128]{2,1,0:T(8,128)} %source_hbm.1, f32[6,48,128]{2,1,0:T(8,128)} %cot_hbm.1, f32[2,48,128]{2,1,0:T(8,128)} %coef_hbm.1, s32[6,48,128]{2,1,0:T(8,128)} %mask_hbm.1, ...), custom_call_target="tpu_custom_call" | custom-call | tf_op jit(solution)/shard_map/window/pallas_call | solution.py:366
  33.2 0.8 %store.1 = (f32[6,48,128]{2,1,0:T(8,128)}, f32[6,48,128]{2,1,0:T(8,128)}, f32[6,48,128]{2,1,0:T(8,128)}) custom-call(f32[6,48,128]{2,1,0:T(8,128)S(1)} %get-tuple-element.6.a_ref, f32[6,48,128]{2,1,0:T(8,128)S(1)} %get-tuple-element.7.b_ref, f32[6,48,128]{2,1,0:T(8,128)S(1)} %get-tuple-element.8.c_ref), custom_call_target="tpu_custom_call" | custom-call | tf_op jit(solution)/shard_map/store/pallas_call | solution.py:390

commit v3 on v2

v3 whole, which is shorter than its diff:
```python
import jax
import jax.numpy as jnp
from jax import lax
from jax.experimental import pallas as pl
from jax.experimental.pallas import tpu as pltpu
from jax.sharding import PartitionSpec as P

MESH = pl.DeviceIdType.MESH
STEPS = 4
K = 6
ROWS = 48
LANES = 128
TILES = 8
PAD = 80
GROUP = 7
COEF_UNROLL = 2
VERTICAL = 0.04
F32 = jnp.float32

STATE, WET, COEF, SOURCE, COT, OTHER = 0, 6, 12, 14, 20, 26
PLANES = 26
FRINGE = 4
PAIRS = PLANES // 2 + 1


def lane_roll(x, shift):
    if isinstance(shift, int):
        shift %= LANES
    return pltpu.roll(x, shift, x.ndim - 1)


def kernel(
    state_hbm, source_hbm, cot_hbm, coef_hbm, mask_hbm, bottom_hbm,
    final_ref, gini_ref, gsrc_ref,
    x_ref, mask, bottom,
    c_e, c_w, c_edge, c_n, c_z, diag, gain, adj,
    packed, pack_e, pack_w, corner_out, got_w, got_e, corner_in,
    s_ref, s_c, s_gain,
    load_sem, send_sem, recv_sem,
):
    lat, lon = lax.axis_index("lat"), lax.axis_index("lon")
    n_lat, n_lon = lax.axis_size("lat"), lax.axis_size("lon")
    up, down = lax.rem(lat + 1, n_lat), lax.rem(lat + n_lat - 1, n_lat)
    east, west = lax.rem(lon + 1, n_lon), lax.rem(lon + n_lon - 1, n_lon)
    has_up, has_down = lat < n_lat - 1, lat > 0

    barrier = pltpu.get_barrier_semaphore()

    def greet(devices):
        for device in devices:
            pl.semaphore_signal(barrier, inc=1, device_id=device, device_id_type=MESH)

    greet([(lat, east), (lat, west)])
    pl.when(has_up)(lambda: greet([(up, lon), (up, east), (up, west)]))
    pl.when(has_down)(lambda: greet([(down, lon), (down, east), (down, west)]))

    lane = lax.broadcasted_iota(jnp.int32, (1, 8, LANES), 2)
    sub = lax.broadcasted_iota(jnp.int32, (1, 8, LANES), 1)
    block = lane // 16
    left = lane % 16 < 8

    def planes(start, count):
        return x_ref.at[pl.ds(start, count)]

    fields = [
        (mask_hbm, mask, 8, 8),
        (bottom_hbm, bottom, 8, 8),
        (coef_hbm, planes(COEF, 2), 16, 8),
        (state_hbm, planes(STATE, K), 16, 8),
        (source_hbm, planes(SOURCE, K), 16, 8),
        (cot_hbm, planes(COT, K), 16, FRINGE),
    ]
    urgent, later_fields = range(4), range(4, 6)

    def rows_of(ref, start, size):
        if len(ref.shape) == 2:
            return ref.at[pl.ds(start, size)]
        return ref.at[:, pl.ds(start, size)]

    loads = [
        pltpu.make_async_copy(hbm, rows_of(ref, first, ROWS), load_sem.at[i])
        for i, (hbm, ref, first, _) in enumerate(fields)
    ]
    for load in loads:
        load.start()

    def remote(src_ref, dst_ref, i, device):
        return pltpu.make_async_remote_copy(
            src_ref=src_ref, dst_ref=dst_ref, send_sem=send_sem.at[i], recv_sem=recv_sem.at[i],
            device_id=device, device_id_type=MESH,
        )

    rows_up = [
        remote(rows_of(hbm, ROWS - size, size), rows_of(ref, first - size, size), i, (up, lon))
        for i, (hbm, ref, first, size) in enumerate(fields)
    ]
    rows_down = [
        remote(rows_of(hbm, 0, size), rows_of(ref, first + ROWS, size), 6 + i, (down, lon))
        for i, (hbm, ref, first, size) in enumerate(fields)
    ]

    def strip_copies(g):
        part = pl.ds(GROUP * g, GROUP)
        return [
            remote(pack_e.at[part], got_w.at[part], 12 + g, (lat, east)),
            remote(pack_w.at[part], got_e.at[part], 14 + g, (lat, west)),
        ]

    def corners_up(g):
        return [
            remote(corner_out.at[c, g], corner_in.at[c, g], 16 + 2 * c + g, (up, side))
            for c, side in ((0, east), (1, west))
        ]

    def corners_down(g):
        return [
            remote(corner_out.at[c, g], corner_in.at[c, g], 16 + 2 * c + g, (down, side))
            for c, side in ((2, east), (3, west))
        ]

    def start(copies):
        for copy in copies:
            copy.start()

    def received(copies):
        for copy in copies:
            copy.wait_recv()

    def sent(copies):
        for copy in copies:
            copy.wait_send()

    zero_tile = jnp.zeros((1, 8, LANES), F32)

    def clear(p, carry):
        x_ref[pl.ds(p, 1), 0:8] = zero_tile
        x_ref[pl.ds(p, 1), 72:80] = zero_tile
        return carry

    lax.fori_loop(0, PLANES + K, clear, 0)
    c_n[:, 0:8] = jnp.zeros((K, 8, LANES), F32)
    x_ref[COT : COT + K, 8 : 16 - FRINGE] = jnp.zeros((K, 8 - FRINGE, LANES), F32)
    x_ref[COT : COT + K, 64 + FRINGE : 72] = jnp.zeros((K, 8 - FRINGE, LANES), F32)

    def beyond_pole(rows, corner):
        x_ref[0:PLANES, rows : rows + 8] = jnp.zeros((PLANES, 8, LANES), F32)
        corner_in[corner : corner + 2] = jnp.zeros((2, 2, 8, LANES), F32)

    pl.when(jnp.logical_not(has_down))(lambda: beyond_pole(8, 0))
    pl.when(jnp.logical_not(has_up))(lambda: beyond_pole(64, 2))

    pl.semaphore_wait(barrier, 2 + 3 * (has_up.astype(jnp.int32) + has_down.astype(jnp.int32)))

    pl.when(has_up)(lambda: start([rows_up[i] for i in urgent]))
    pl.when(has_down)(lambda: start([rows_down[i] for i in urgent]))

    def wet_rows(first, size):
        for k in range(K):
            here = pl.ds(first, size)
            x_ref[WET + k, pl.ds(first + 8, size)] = jnp.where(k < bottom[here], mask[k, here], 0).astype(F32)

    def pack(g, j):
        i = GROUP * g + j
        both = []
        for q in range(2):
            total = zero_tile
            for t in range(6):
                moved = lane_roll(x_ref[pl.ds(2 * i + q, 1), 16 + 8 * t : 24 + 8 * t], 16 * (t + 1) + 8)
                total = moved if t == 0 else jnp.where(block == t + 1, moved, total)
            packed[pl.ds(2 * i + q, 1)] = total
            both.append(total)
        to_east = jnp.where(left, both[0], lane_roll(both[1], 8))
        to_west = jnp.where(left, lane_roll(both[0], -8), both[1])
        pack_e[pl.ds(i, 1)] = to_east
        pack_w[pl.ds(i, 1)] = to_west
        return [
            lane_roll(value, 16 * (j - source_block))
            for value, source_block in ((to_east, 6), (to_west, 6), (to_east, 1), (to_west, 1))
        ]

    def pack_group(g, carry):
        @pl.when(g == 0)
        def _():
            for i in urgent:
                loads[i].wait()
            wet_rows(8, ROWS)

        @pl.when(g == 1)
        def _():
            for i in later_fields:
                loads[i].wait()

        corner = [zero_tile] * 4
        for j in range(GROUP):
            corner = [jnp.where(block == j, new, old) for new, old in zip(pack(g, j), corner)]
        for c in range(4):
            corner_out[c, pl.ds(g, 1)] = corner[c]
        start(strip_copies(g))
        pl.when(has_up)(lambda: start(corners_up(g)))
        pl.when(has_down)(lambda: start(corners_down(g)))
        return carry

    lax.fori_loop(0, 2, pack_group, 0)
    pl.when(has_up)(lambda: start([rows_up[i] for i in later_fields]))
    pl.when(has_down)(lambda: start([rows_down[i] for i in later_fields]))

    def unpack(g, j):
        i = GROUP * g + j
        sides = []
        for ref, low, high in ((got_w, 0, 2), (got_e, 1, 3)):
            total = ref[pl.ds(i, 1)]
            total = jnp.where(block == 0, lane_roll(corner_in[low, pl.ds(g, 1)], -16 * j), total)
            total = jnp.where(block == 7, lane_roll(corner_in[high, pl.ds(g, 1)], 16 * (7 - j)), total)
            sides.append(total)
        from_west, from_east = sides
        for q in range(2):
            p = 2 * i + q
            mine = packed[pl.ds(p, 1)]
            mine = jnp.where(block == 0, lane_roll(x_ref[pl.ds(p, 1), 8:16], 8), mine)
            mine = jnp.where(block == 7, lane_roll(x_ref[pl.ds(p, 1), 64:72], 120), mine)
            a = from_west if q == 0 else lane_roll(from_west, -8)
            b = lane_roll(from_east, 8) if q == 0 else from_east
            s_ref[pl.ds(2 * p, 1)] = jnp.where(left, a, mine)
            s_ref[pl.ds(2 * p + 1, 1)] = jnp.where(left, mine, b)

    def s_north(x):
        rolled = pltpu.roll(x, 7, 1)
        return jnp.where(sub == 7, lane_roll(rolled, -16), rolled)

    def s_south(x):
        rolled = pltpu.roll(x, 1, 1)
        return jnp.where(sub == 0, lane_roll(rolled, 16), rolled)

    def beside(x, a, b, r):
        turned = lane_roll(jnp.where(left, a, b), lax.rem(120 + LANES - 16 * r, LANES))
        return (
            lane_roll(jnp.where(lane == 0, turned, x), -1),
            lane_roll(jnp.where(lane == LANES - 1, turned, x), 1),
        )

    def level(p):
        return s_ref[2 * p : 2 * p + 1], s_ref[2 * p + 1 : 2 * p + 2]

    def by_tile(count, unroll, one):
        def several(i, carry):
            for q in range(unroll):
                r = i * unroll + q
                one(r, pl.multiple_of(8 * r, 8))
            return carry

        lax.fori_loop(0, count // unroll, several, 0)

    nothing = jnp.zeros((2, 8, LANES), F32)

    def strip_coefficients():
        def six(pair):
            return jnp.concatenate([pair] * K, 0)

        w = s_ref[2 * WET : 2 * WET + 2 * K]
        all_e = six(s_ref[2 * COEF : 2 * COEF + 2])
        all_n = six(s_ref[2 * COEF + 2 : 2 * COEF + 4])
        s_ce = all_e * w * lane_roll(w, -1)
        s_cw = lane_roll(all_e, 1) * lane_roll(w, 1) * w
        s_cn = all_n * w * s_north(w)
        s_cs = s_south(all_n) * s_south(w) * w
        s_cz = VERTICAL * (w[:-2] * w[2:])
        s_d = 1.0 - (s_ce + s_cw) - (s_cn + s_cs)
        s_d = s_d - jnp.concatenate([s_cz, nothing], 0) - jnp.concatenate([nothing, s_cz], 0)
        for i, part in enumerate((s_d, s_ce, s_cw, s_cn, s_cs)):
            s_c[i] = part
        s_c[5, 0:10] = s_cz

    def coefficients(r, t):
        here, at = pl.ds(t, 8), pl.ds(t + 8, 8)
        ce, cn = x_ref[COEF : COEF + 1, at], x_ref[COEF + 1 : COEF + 2, at]
        cs = x_ref[COEF + 1 : COEF + 2, pl.ds(t + 7, 8)]
        _, ce_west = beside(ce, *level(COEF), r)
        tiles = [x_ref[WET + k : WET + k + 1, at] for k in range(K)]
        below = None
        for k in range(K):
            wk = tiles[k]
            w_east, w_west = beside(wk, *level(WET + k), r)
            e, wst = ce * wk * w_east, ce_west * w_west * wk
            n = cn * wk * x_ref[WET + k : WET + k + 1, pl.ds(t + 9, 8)]
            s = cs * x_ref[WET + k : WET + k + 1, pl.ds(t + 7, 8)] * wk
            d = 1.0 - (e + wst) - (n + s)
            if k < K - 1:
                z = VERTICAL * (wk * tiles[k + 1])
                c_z[k : k + 1, here] = z
                d = d - z
            if below is not None:
                d = d - below
            below = z
            first, last = lane == 0, lane == LANES - 1
            c_e[k : k + 1, here] = jnp.where(last, 0.0, e)
            c_w[k : k + 1, here] = jnp.where(first, 0.0, wst)
            c_edge[k : k + 1, here] = jnp.where(first, wst, jnp.where(last, e, 0.0))
            c_n[k : k + 1, at] = n
            diag[k : k + 1, here] = d

    def unpack_group(g, carry):
        @pl.when(g == 0)
        def _():
            pl.when(has_down)(lambda: received([rows_up[i] for i in urgent]))
            pl.when(has_up)(lambda: received([rows_down[i] for i in urgent]))
            pl.when(has_down)(lambda: wet_rows(0, 8))
            pl.when(has_up)(lambda: wet_rows(ROWS + 8, 8))

        @pl.when(g == 1)
        def _():
            pl.when(has_down)(lambda: received([rows_up[i] for i in later_fields]))
            pl.when(has_up)(lambda: received([rows_down[i] for i in later_fields]))

        received(strip_copies(g))
        pl.when(has_down)(lambda: received(corners_up(g)))
        pl.when(has_up)(lambda: received(corners_down(g)))
        for j in range(GROUP):
            unpack(g, j)

        @pl.when(g == 0)
        def _():
            strip_coefficients()
            by_tile(TILES, COEF_UNROLL, coefficients)

        return carry

    lax.fori_loop(0, 2, unpack_group, 0)

    def strip_product(base):
        x = s_ref[pl.ds(2 * base, 2 * K)]
        x_east, x_west = lane_roll(x, -1), lane_roll(x, 1)
        out = s_c[0] * x + (s_c[1] * x_east + s_c[2] * x_west)
        out = out + (s_c[3] * s_north(x) + s_c[4] * s_south(x))
        cz = s_c[5, 0:10]
        out = out + jnp.concatenate([cz * x[2:], nothing], 0) + jnp.concatenate([nothing, cz * x[:-2]], 0)
        return out, [jnp.where(left, x_east[2 * k + 1 : 2 * k + 2], x_west[2 * k : 2 * k + 1]) for k in range(K)]

    def product(base, edges, r, t):
        here, at = pl.ds(t, 8), pl.ds(t + 8, 8)
        north, south = pl.ds(t + 9, 8), pl.ds(t + 7, 8)
        x = [x_ref[pl.ds(base + k, 1), at] for k in range(K)]
        out = []
        for k in range(K):
            one = pl.ds(base + k, 1)
            edge = lane_roll(edges[k], 120 - 16 * r)
            p = c_e[k : k + 1, here] * lane_roll(x[k], -1) + c_w[k : k + 1, here] * lane_roll(x[k], 1)
            p = p + (c_edge[k : k + 1, here] * edge + diag[k : k + 1, here] * x[k])
            p = p + (c_n[k : k + 1, at] * x_ref[one, north] + c_n[k : k + 1, south] * x_ref[one, south])
            if k < K - 1:
                p = p + c_z[k : k + 1, here] * x[k + 1]
            if k > 0:
                p = p + c_z[k - 1 : k, here] * x[k - 1]
            out.append(p)
        return out

    def all_tiles(one):
        for r in range(TILES):
            one(r, 8 * r)

    def forward(n, carry):
        now = OTHER * lax.rem(n, 2)
        later = OTHER - now
        p, edges = strip_product(now)
        bounded = jnp.tanh(p)
        s_gain[n] = 1.0 - bounded * bounded
        s_ref[pl.ds(2 * later, 2 * K)] = bounded + s_ref[2 * SOURCE : 2 * SOURCE + 2 * K]

        def one(r, t):
            for k, p in enumerate(product(now, edges, r, t)):
                bounded = jnp.tanh(p)
                gain[n, k : k + 1, pl.ds(t, 8)] = 1.0 - bounded * bounded
                at = pl.ds(t + 8, 8)
                x_ref[pl.ds(later + k, 1), at] = bounded + x_ref[SOURCE + k : SOURCE + k + 1, at]

        all_tiles(one)
        return carry

    lax.fori_loop(0, STEPS, forward, 0)

    def turn(k, carry):
        one, o = pl.ds(k, 1), pl.ds(16, ROWS)
        final_ref[one] = x_ref[pl.ds(WET + k, 1), o] * x_ref[pl.ds(STATE + k, 1), o]
        x_ref[one, 8:72] = gain[STEPS - 1, one] * x_ref[pl.ds(COT + k, 1), 8:72]
        return carry

    lax.fori_loop(0, K, turn, 0)
    s_ref[0 : 2 * K] = s_gain[STEPS - 1] * s_ref[2 * COT : 2 * COT + 2 * K]

    def backward(m, carry):
        n = STEPS - 1 - m
        before = jnp.maximum(n - 1, 0)
        now = OTHER * lax.rem(m, 2)
        later = OTHER - now
        p, edges = strip_product(now)
        s_ref[pl.ds(2 * later, 2 * K)] = s_gain[before] * p

        def one(r, t):
            for k, p in enumerate(product(now, edges, r, t)):
                here = pl.ds(t, 8)
                adj[n, k : k + 1, here] = p
                x_ref[pl.ds(later + k, 1), pl.ds(t + 8, 8)] = gain[before, k : k + 1, here] * p

        all_tiles(one)
        return carry

    lax.fori_loop(0, STEPS, backward, 0)

    def finish(k, carry):
        one, o = pl.ds(k, 1), pl.ds(8, ROWS)
        wk = x_ref[pl.ds(WET + k, 1), 16 : 16 + ROWS]
        gini_ref[one] = wk * adj[0, one, o]
        gsrc_ref[one] = wk * (
            x_ref[pl.ds(COT + k, 1), 16 : 16 + ROWS] + adj[1, one, o] + (adj[2, one, o] + adj[3, one, o])
        )
        return carry

    lax.fori_loop(0, K, finish, 0)
    pl.when(has_up)(lambda: sent(rows_up))
    pl.when(has_down)(lambda: sent(rows_down))
    for g in range(2):
        sent(strip_copies(g))
        pl.when(has_up)(lambda: sent(corners_up(g)))
        pl.when(has_down)(lambda: sent(corners_down(g)))


def store(a_ref, b_ref, c_ref, a_out, b_out, c_out, sem):
    copies = [
        pltpu.make_async_copy(src_ref, dst_ref, sem.at[i])
        for i, (src_ref, dst_ref) in enumerate(((a_ref, a_out), (b_ref, b_out), (c_ref, c_out)))
    ]
    for copy in copies:
        copy.start()
    for copy in copies:
        copy.wait()


def body(initial_state, source, cotangent, face_coefs, land_mask, bottom):
    out = pltpu.VMEM((K, ROWS, LANES), F32)
    tiles = pltpu.VMEM((K, 8 * TILES, LANES), F32)
    pairs = pltpu.VMEM((PAIRS, 8, LANES), F32)
    steps = pltpu.VMEM((STEPS, K, 8 * TILES, LANES), F32)
    corner = pltpu.VMEM((4, 2, 8, LANES), F32)
    results = pl.pallas_call(
        kernel,
        name="window",
        out_shape=(out, out, out),
        in_specs=[pl.BlockSpec(memory_space=pl.ANY)] * 6,
        out_specs=(pl.BlockSpec(memory_space=pltpu.VMEM),) * 3,
        scratch_shapes=[
            pltpu.VMEM((PLANES + K, PAD, LANES), F32),
            pltpu.VMEM((K, 8 * TILES, LANES), jnp.int32),
            pltpu.VMEM((8 * TILES, LANES), jnp.int32),
            tiles, tiles, tiles, pltpu.VMEM((K, PAD, LANES), F32), tiles, tiles,
            steps, steps,
            pltpu.VMEM((2 * PAIRS, 8, LANES), F32),
            pairs, pairs, corner, pairs, pairs, corner,
            pltpu.VMEM((2 * (PLANES + K), 8, LANES), F32),
            pltpu.VMEM((6, 2 * K, 8, LANES), F32),
            pltpu.VMEM((STEPS, 2 * K, 8, LANES), F32),
            pltpu.SemaphoreType.DMA((6,)),
            pltpu.SemaphoreType.DMA((24,)),
            pltpu.SemaphoreType.DMA((24,)),
        ],
        compiler_params=pltpu.CompilerParams(collective_id=0, has_side_effects=True),
    )(initial_state, source, cotangent, face_coefs, land_mask, bottom)
    plain = jax.ShapeDtypeStruct((K, ROWS, LANES), F32)
    return pl.pallas_call(
        store,
        name="store",
        out_shape=(plain,) * 3,
        in_specs=[pl.BlockSpec(memory_space=pltpu.VMEM)] * 3,
        out_specs=(pl.BlockSpec(memory_space=pl.ANY),) * 3,
        scratch_shapes=[pltpu.SemaphoreType.DMA((3,))],
    )(*[pltpu.with_memory_space_constraint(x, pltpu.VMEM) for x in results])


def solution(mesh):
    spec = P(None, "lat", "lon")
    return jax.shard_map(
        body,
        mesh=mesh,
        in_specs=(spec,) * 5 + (P("lat", "lon"),),
        out_specs=(spec,) * 3,
        check_vma=False,
    )
```

time: 34.2 us -> 23.7 us (0.69)
  Pallas kernels: 33.4 us -> 22.9 us
    pallas_call x1, Pallas kernels: 32.6 us -> 22.1 us  [body(): pl.pallas_call(kernel, name='window', out_shape=(out, out, out), in_specs...]
where the time goes in v3:
time: 23.7 us; the launch traced here: 23.6 us
  Pallas kernels  22.9 us (97%)
  between operations  0.64 us (3%)
    pallas_call x1, Pallas kernels, body(): pl.pallas_call(kernel, name='window', out_shape=(out, out, out), in_specs...  22.1 us
    pallas_call x1, Pallas kernels, body(): pl.pallas_call(store, name='store', out_shape=(plain,) * 3, in_specs=[pl....  0.79 us

profile of v3, /device:TPU:1, one launch (start us, length us, event | category | flops | bytes accessed | tf_op | source)
XLA Modules:
  0.0 23.6 jit_solution(12594628064543654179)
XLA Ops:
  0.6 22.1 %window.1 = (f32[6,48,128]{2,1,0:T(8,128)S(1)}, f32[6,48,128]{2,1,0:T(8,128)S(1)}, f32[6,48,128]{2,1,0:T(8,128)S(1)}) custom-call(f32[6,48,128]{2,1,0:T(8,128)} %state_hbm.1, f32[6,48,128]{2,1,0:T(8,128)} %source_hbm.1, f32[6,48,128]{2,1,0:T(8,128)} %cot_hbm.1, f32[2,48,128]{2,1,0:T(8,128)} %coef_hbm.1, s32[6,48,128]{2,1,0:T(8,128)} %mask_hbm.1, ...), custom_call_target="tpu_custom_call" | custom-call | tf_op jit(solution)/shard_map/window/pallas_call | solution.py:443
  22.8 0.8 %store.1 = (f32[6,48,128]{2,1,0:T(8,128)}, f32[6,48,128]{2,1,0:T(8,128)}, f32[6,48,128]{2,1,0:T(8,128)}) custom-call(f32[6,48,128]{2,1,0:T(8,128)S(1)} %get-tuple-element.6.a_ref, f32[6,48,128]{2,1,0:T(8,128)S(1)} %get-tuple-element.7.b_ref, f32[6,48,128]{2,1,0:T(8,128)S(1)} %get-tuple-element.8.c_ref), custom_call_target="tpu_custom_call" | custom-call | tf_op jit(solution)/shard_map/store/pallas_call | solution.py:467

commit v4 on v3

--- a/solution.py
+++ b/solution.py
@@ -13,7 +13,6 @@
 TILES = 8
 PAD = 80
 GROUP = 7
-COEF_UNROLL = 2
 VERTICAL = 0.04
 F32 = jnp.float32
 
@@ -62,24 +61,22 @@
     def planes(start, count):
         return x_ref.at[pl.ds(start, count)]
 
-    fields = [
-        (mask_hbm, mask, 8, 8),
-        (bottom_hbm, bottom, 8, 8),
-        (coef_hbm, planes(COEF, 2), 16, 8),
-        (state_hbm, planes(STATE, K), 16, 8),
-        (source_hbm, planes(SOURCE, K), 16, 8),
-        (cot_hbm, planes(COT, K), 16, FRINGE),
-    ]
-    urgent, later_fields = range(4), range(4, 6)
-
     def rows_of(ref, start, size):
-        if len(ref.shape) == 2:
-            return ref.at[pl.ds(start, size)]
         return ref.at[:, pl.ds(start, size)]
 
+    own = pl.ds(16, ROWS)
     loads = [
-        pltpu.make_async_copy(hbm, rows_of(ref, first, ROWS), load_sem.at[i])
-        for i, (hbm, ref, first, _) in enumerate(fields)
+        pltpu.make_async_copy(hbm, ref, load_sem.at[i])
+        for i, (hbm, ref) in enumerate(
+            [
+                (bottom_hbm, bottom),
+                (mask_hbm, mask),
+                (coef_hbm, x_ref.at[COEF : COEF + 2, own]),
+                (state_hbm, x_ref.at[STATE : STATE + K, own]),
+                (source_hbm, x_ref.at[SOURCE : SOURCE + K, own]),
+                (cot_hbm, x_ref.at[COT : COT + K, own]),
+            ]
+        )
     ]
     for load in loads:
         load.start()
@@ -90,31 +87,31 @@
             device_id=device, device_id_type=MESH,
         )
 
+    parts = [(planes(0, SOURCE), 8), (planes(SOURCE, K), 8), (planes(COT, K), FRINGE)]
     rows_up = [
-        remote(rows_of(hbm, ROWS - size, size), rows_of(ref, first - size, size), i, (up, lon))
-        for i, (hbm, ref, first, size) in enumerate(fields)
+        remote(rows_of(ref, 64 - size, size), rows_of(ref, 16 - size, size), i, (up, lon))
+        for i, (ref, size) in enumerate(parts)
     ]
     rows_down = [
-        remote(rows_of(hbm, 0, size), rows_of(ref, first + ROWS, size), 6 + i, (down, lon))
-        for i, (hbm, ref, first, size) in enumerate(fields)
+        remote(rows_of(ref, 16, size), rows_of(ref, 64, size), 3 + i, (down, lon)) for i, (ref, size) in enumerate(parts)
     ]
 
     def strip_copies(g):
         part = pl.ds(GROUP * g, GROUP)
         return [
-            remote(pack_e.at[part], got_w.at[part], 12 + g, (lat, east)),
-            remote(pack_w.at[part], got_e.at[part], 14 + g, (lat, west)),
+            remote(pack_e.at[part], got_w.at[part], 6 + g, (lat, east)),
+            remote(pack_w.at[part], got_e.at[part], 8 + g, (lat, west)),
         ]
 
     def corners_up(g):
         return [
-            remote(corner_out.at[c, g], corner_in.at[c, g], 16 + 2 * c + g, (up, side))
+            remote(corner_out.at[c, g], corner_in.at[c, g], 10 + 2 * c + g, (up, side))
             for c, side in ((0, east), (1, west))
         ]
 
     def corners_down(g):
         return [
-            remote(corner_out.at[c, g], corner_in.at[c, g], 16 + 2 * c + g, (down, side))
+            remote(corner_out.at[c, g], corner_in.at[c, g], 10 + 2 * c + g, (down, side))
             for c, side in ((2, east), (3, west))
         ]
 
@@ -132,32 +129,9 @@
 
     zero_tile = jnp.zeros((1, 8, LANES), F32)
 
-    def clear(p, carry):
-        x_ref[pl.ds(p, 1), 0:8] = zero_tile
-        x_ref[pl.ds(p, 1), 72:80] = zero_tile
-        return carry
-
-    lax.fori_loop(0, PLANES + K, clear, 0)
-    c_n[:, 0:8] = jnp.zeros((K, 8, LANES), F32)
-    x_ref[COT : COT + K, 8 : 16 - FRINGE] = jnp.zeros((K, 8 - FRINGE, LANES), F32)
-    x_ref[COT : COT + K, 64 + FRINGE : 72] = jnp.zeros((K, 8 - FRINGE, LANES), F32)
-
-    def beyond_pole(rows, corner):
-        x_ref[0:PLANES, rows : rows + 8] = jnp.zeros((PLANES, 8, LANES), F32)
-        corner_in[corner : corner + 2] = jnp.zeros((2, 2, 8, LANES), F32)
-
-    pl.when(jnp.logical_not(has_down))(lambda: beyond_pole(8, 0))
-    pl.when(jnp.logical_not(has_up))(lambda: beyond_pole(64, 2))
-
-    pl.semaphore_wait(barrier, 2 + 3 * (has_up.astype(jnp.int32) + has_down.astype(jnp.int32)))
-
-    pl.when(has_up)(lambda: start([rows_up[i] for i in urgent]))
-    pl.when(has_down)(lambda: start([rows_down[i] for i in urgent]))
-
-    def wet_rows(first, size):
+    def wet_cells():
         for k in range(K):
-            here = pl.ds(first, size)
-            x_ref[WET + k, pl.ds(first + 8, size)] = jnp.where(k < bottom[here], mask[k, here], 0).astype(F32)
+            x_ref[WET + k, own] = jnp.where(k < bottom[...], mask[k], 0).astype(F32)
 
     def pack(g, j):
         i = GROUP * g + j
@@ -181,13 +155,13 @@
     def pack_group(g, carry):
         @pl.when(g == 0)
         def _():
-            for i in urgent:
+            for i in range(4):
                 loads[i].wait()
-            wet_rows(8, ROWS)
+            wet_cells()
 
         @pl.when(g == 1)
         def _():
-            for i in later_fields:
+            for i in range(4, 6):
                 loads[i].wait()
 
         corner = [zero_tile] * 4
@@ -195,14 +169,37 @@
             corner = [jnp.where(block == j, new, old) for new, old in zip(pack(g, j), corner)]
         for c in range(4):
             corner_out[c, pl.ds(g, 1)] = corner[c]
-        start(strip_copies(g))
+        return carry
+
+    lax.fori_loop(0, 2, pack_group, 0)
+    pl.semaphore_wait(barrier, 2 + 3 * (has_up.astype(jnp.int32) + has_down.astype(jnp.int32)))
+
+    def send_group(g, up_rows, down_rows):
         pl.when(has_up)(lambda: start(corners_up(g)))
         pl.when(has_down)(lambda: start(corners_down(g)))
-        return carry
-
-    lax.fori_loop(0, 2, pack_group, 0)
-    pl.when(has_up)(lambda: start([rows_up[i] for i in later_fields]))
-    pl.when(has_down)(lambda: start([rows_down[i] for i in later_fields]))
+        start(strip_copies(g))
+        pl.when(has_up)(lambda: start(up_rows))
+        pl.when(has_down)(lambda: start(down_rows))
+
+    send_group(0, rows_up[:1], rows_down[:1])
+    send_group(1, rows_up[1:], rows_down[1:])
+
+    def clear(p, carry):
+        x_ref[pl.ds(p, 1), 0:8] = zero_tile
+        x_ref[pl.ds(p, 1), 72:80] = zero_tile
+        return carry
+
+    lax.fori_loop(0, PLANES + K, clear, 0)
+    c_n[:, 0:8] = jnp.zeros((K, 8, LANES), F32)
+    x_ref[COT : COT + K, 8 : 16 - FRINGE] = jnp.zeros((K, 8 - FRINGE, LANES), F32)
+    x_ref[COT : COT + K, 64 + FRINGE : 72] = jnp.zeros((K, 8 - FRINGE, LANES), F32)
+
+    def beyond_pole(rows, corner):
+        x_ref[0:PLANES, rows : rows + 8] = jnp.zeros((PLANES, 8, LANES), F32)
+        corner_in[corner : corner + 2] = jnp.zeros((2, 2, 8, LANES), F32)
+
+    pl.when(jnp.logical_not(has_down))(lambda: beyond_pole(8, 0))
+    pl.when(jnp.logical_not(has_up))(lambda: beyond_pole(64, 2))
 
     def unpack(g, j):
         i = GROUP * g + j
@@ -231,25 +228,6 @@
         rolled = pltpu.roll(x, 1, 1)
         return jnp.where(sub == 0, lane_roll(rolled, 16), rolled)
 
-    def beside(x, a, b, r):
-        turned = lane_roll(jnp.where(left, a, b), lax.rem(120 + LANES - 16 * r, LANES))
-        return (
-            lane_roll(jnp.where(lane == 0, turned, x), -1),
-            lane_roll(jnp.where(lane == LANES - 1, turned, x), 1),
-        )
-
-    def level(p):
-        return s_ref[2 * p : 2 * p + 1], s_ref[2 * p + 1 : 2 * p + 2]
-
-    def by_tile(count, unroll, one):
-        def several(i, carry):
-            for q in range(unroll):
-                r = i * unroll + q
-                one(r, pl.multiple_of(8 * r, 8))
-            return carry
-
-        lax.fori_loop(0, count // unroll, several, 0)
-
     nothing = jnp.zeros((2, 8, LANES), F32)
 
     def strip_coefficients():
@@ -270,17 +248,18 @@
             s_c[i] = part
         s_c[5, 0:10] = s_cz
 
-    def coefficients(r, t):
+    def coefficients(r):
+        t = pl.multiple_of(8 * r, 8)
         here, at = pl.ds(t, 8), pl.ds(t + 8, 8)
         ce, cn = x_ref[COEF : COEF + 1, at], x_ref[COEF + 1 : COEF + 2, at]
         cs = x_ref[COEF + 1 : COEF + 2, pl.ds(t + 7, 8)]
-        _, ce_west = beside(ce, *level(COEF), r)
+        ce = jnp.where(lane == LANES - 1, 0.0, ce)
         tiles = [x_ref[WET + k : WET + k + 1, at] for k in range(K)]
         below = None
         for k in range(K):
             wk = tiles[k]
-            w_east, w_west = beside(wk, *level(WET + k), r)
-            e, wst = ce * wk * w_east, ce_west * w_west * wk
+            e = ce * (wk * lane_roll(wk, -1))
+            wst = lane_roll(e, 1)
             n = cn * wk * x_ref[WET + k : WET + k + 1, pl.ds(t + 9, 8)]
             s = cs * x_ref[WET + k : WET + k + 1, pl.ds(t + 7, 8)] * wk
             d = 1.0 - (e + wst) - (n + s)
@@ -291,40 +270,58 @@
             if below is not None:
                 d = d - below
             below = z
-            first, last = lane == 0, lane == LANES - 1
-            c_e[k : k + 1, here] = jnp.where(last, 0.0, e)
-            c_w[k : k + 1, here] = jnp.where(first, 0.0, wst)
-            c_edge[k : k + 1, here] = jnp.where(first, wst, jnp.where(last, e, 0.0))
+            c_e[k : k + 1, here] = e
+            c_w[k : k + 1, here] = wst
             c_n[k : k + 1, at] = n
             diag[k : k + 1, here] = d
 
+    edge_lane = jnp.logical_or(lane == 0, lane == LANES - 1)
+
+    def edge_coefficients(k, carry):
+        one = pl.ds(k, 1)
+        faces = jnp.where(left, s_c[1, pl.ds(2 * k + 1, 1)], s_c[2, pl.ds(2 * k, 1)])
+        for r in range(TILES):
+            here = pl.ds(8 * r, 8)
+            c = jnp.where(edge_lane, lane_roll(faces, 120 - 16 * r), 0.0)
+            c_edge[one, here] = c
+            diag[one, here] = diag[one, here] - c
+        return carry
+
     def unpack_group(g, carry):
-        @pl.when(g == 0)
-        def _():
-            pl.when(has_down)(lambda: received([rows_up[i] for i in urgent]))
-            pl.when(has_up)(lambda: received([rows_down[i] for i in urgent]))
-            pl.when(has_down)(lambda: wet_rows(0, 8))
-            pl.when(has_up)(lambda: wet_rows(ROWS + 8, 8))
-
-        @pl.when(g == 1)
-        def _():
-            pl.when(has_down)(lambda: received([rows_up[i] for i in later_fields]))
-            pl.when(has_up)(lambda: received([rows_down[i] for i in later_fields]))
-
         received(strip_copies(g))
         pl.when(has_down)(lambda: received(corners_up(g)))
         pl.when(has_up)(lambda: received(corners_down(g)))
         for j in range(GROUP):
             unpack(g, j)
-
-        @pl.when(g == 0)
+        return carry
+
+    def coefficient_group(i, carry):
+        @pl.when(i == 2)
+        def _():
+            pl.when(has_down)(lambda: received(rows_up[:1]))
+            pl.when(has_up)(lambda: received(rows_down[:1]))
+
+        pair = lax.rem(i + 1, 3) + 2 * (i // 3)
+        for q in range(2):
+            coefficients(2 * pair + q)
+        return carry
+
+    lax.fori_loop(0, 4, coefficient_group, 0)
+
+    def finish_group(g, carry):
+        @pl.when(g == 1)
         def _():
             strip_coefficients()
-            by_tile(TILES, COEF_UNROLL, coefficients)
-
-        return carry
-
-    lax.fori_loop(0, 2, unpack_group, 0)
+            lax.fori_loop(0, K, edge_coefficients, 0)
+            pl.when(has_down)(lambda: received(rows_up[1:]))
+            pl.when(has_up)(lambda: received(rows_down[1:]))
+
+        return unpack_group(g, carry)
+
+    lax.fori_loop(0, 2, finish_group, 0)
+
+    pl.when(has_up)(lambda: sent(rows_up[:1]))
+    pl.when(has_down)(lambda: sent(rows_down[:1]))
 
     def strip_product(base):
         x = s_ref[pl.ds(2 * base, 2 * K)]
@@ -415,8 +412,8 @@
         return carry
 
     lax.fori_loop(0, K, finish, 0)
-    pl.when(has_up)(lambda: sent(rows_up))
-    pl.when(has_down)(lambda: sent(rows_down))
+    pl.when(has_up)(lambda: sent(rows_up[1:]))
+    pl.when(has_down)(lambda: sent(rows_down[1:]))
     for g in range(2):
         sent(strip_copies(g))
         pl.when(has_up)(lambda: sent(corners_up(g)))
@@ -448,8 +445,8 @@
         out_specs=(pl.BlockSpec(memory_space=pltpu.VMEM),) * 3,
         scratch_shapes=[
             pltpu.VMEM((PLANES + K, PAD, LANES), F32),
-            pltpu.VMEM((K, 8 * TILES, LANES), jnp.int32),
-            pltpu.VMEM((8 * TILES, LANES), jnp.int32),
+            pltpu.VMEM((K, ROWS, LANES), jnp.int32),
+            pltpu.VMEM((ROWS, LANES), jnp.int32),
             tiles, tiles, tiles, pltpu.VMEM((K, PAD, LANES), F32), tiles, tiles,
             steps, steps,
             pltpu.VMEM((2 * PAIRS, 8, LANES), F32),
@@ -458,8 +455,8 @@
             pltpu.VMEM((6, 2 * K, 8, LANES), F32),
             pltpu.VMEM((STEPS, 2 * K, 8, LANES), F32),
             pltpu.SemaphoreType.DMA((6,)),
-            pltpu.SemaphoreType.DMA((24,)),
-            pltpu.SemaphoreType.DMA((24,)),
+            pltpu.SemaphoreType.DMA((18,)),
+            pltpu.SemaphoreType.DMA((18,)),
         ],
         compiler_params=pltpu.CompilerParams(collective_id=0, has_side_effects=True),
     )(initial_state, source, cotangent, face_coefs, land_mask, bottom)

time: 23.7 us -> 22.8 us (0.962)
  Pallas kernels: 22.9 us -> 22 us
    pallas_call x1, Pallas kernels: 22.1 us -> 21.2 us  [body(): pl.pallas_call(kernel, name='window', out_shape=(out, out, out), in_specs...]
where the time goes in v4:
time: 22.8 us; the launch traced here: 22.6 us
  Pallas kernels  22 us (96%)
  between operations  0.64 us (3%)
    pallas_call x1, Pallas kernels, body(): pl.pallas_call(kernel, name='window', out_shape=(out, out, out), in_specs...  21.2 us
    pallas_call x1, Pallas kernels, body(): pl.pallas_call(store, name='store', out_shape=(plain,) * 3, in_specs=[pl....  0.79 us

profile of v4, /device:TPU:1, one launch (start us, length us, event | category | flops | bytes accessed | tf_op | source)
XLA Modules:
  0.0 22.6 jit_solution(2302537447525945825)
XLA Ops:
  0.6 21.2 %window.1 = (f32[6,48,128]{2,1,0:T(8,128)S(1)}, f32[6,48,128]{2,1,0:T(8,128)S(1)}, f32[6,48,128]{2,1,0:T(8,128)S(1)}) custom-call(f32[6,48,128]{2,1,0:T(8,128)} %state_hbm.1, f32[6,48,128]{2,1,0:T(8,128)} %source_hbm.1, f32[6,48,128]{2,1,0:T(8,128)} %cot_hbm.1, f32[2,48,128]{2,1,0:T(8,128)} %coef_hbm.1, s32[6,48,128]{2,1,0:T(8,128)} %mask_hbm.1, ...), custom_call_target="tpu_custom_call" | custom-call | tf_op jit(solution)/shard_map/window/pallas_call | solution.py:440
  21.8 0.8 %store.1 = (f32[6,48,128]{2,1,0:T(8,128)}, f32[6,48,128]{2,1,0:T(8,128)}, f32[6,48,128]{2,1,0:T(8,128)}) custom-call(f32[6,48,128]{2,1,0:T(8,128)S(1)} %get-tuple-element.6.a_ref, f32[6,48,128]{2,1,0:T(8,128)S(1)} %get-tuple-element.7.b_ref, f32[6,48,128]{2,1,0:T(8,128)S(1)} %get-tuple-element.8.c_ref), custom_call_target="tpu_custom_call" | custom-call | tf_op jit(solution)/shard_map/store/pallas_call | solution.py:464

commit v5 on v4

--- a/solution.py
+++ b/solution.py
@@ -87,7 +87,7 @@
             device_id=device, device_id_type=MESH,
         )
 
-    parts = [(planes(0, SOURCE), 8), (planes(SOURCE, K), 8), (planes(COT, K), FRINGE)]
+    parts = [(planes(0, SOURCE), 8), (planes(SOURCE, K), 7), (planes(COT, K), FRINGE)]
     rows_up = [
         remote(rows_of(ref, 64 - size, size), rows_of(ref, 16 - size, size), i, (up, lon))
         for i, (ref, size) in enumerate(parts)
@@ -191,6 +191,8 @@
 
     lax.fori_loop(0, PLANES + K, clear, 0)
     c_n[:, 0:8] = jnp.zeros((K, 8, LANES), F32)
+    x_ref[SOURCE : SOURCE + K, 8:9] = jnp.zeros((K, 1, LANES), F32)
+    x_ref[SOURCE : SOURCE + K, 71:72] = jnp.zeros((K, 1, LANES), F32)
     x_ref[COT : COT + K, 8 : 16 - FRINGE] = jnp.zeros((K, 8 - FRINGE, LANES), F32)
     x_ref[COT : COT + K, 64 + FRINGE : 72] = jnp.zeros((K, 8 - FRINGE, LANES), F32)
 

time: 22.8 us -> 22.7 us (level)
  no operation moved by 1% of the time
where the time goes in v5:
time: 22.7 us; the launch traced here: 22.5 us
  Pallas kernels  21.9 us (96%)
  between operations  0.64 us (3%)
    pallas_call x1, Pallas kernels, body(): pl.pallas_call(kernel, name='window', out_shape=(out, out, out), in_specs...  21.1 us
    pallas_call x1, Pallas kernels, body(): pl.pallas_call(store, name='store', out_shape=(plain,) * 3, in_specs=[pl....  0.79 us

profile of v5, /device:TPU:1, one launch (start us, length us, event | category | flops | bytes accessed | tf_op | source)
XLA Modules:
  0.0 22.5 jit_solution(12204740059944185677)
XLA Ops:
  0.6 21.1 %window.1 = (f32[6,48,128]{2,1,0:T(8,128)S(1)}, f32[6,48,128]{2,1,0:T(8,128)S(1)}, f32[6,48,128]{2,1,0:T(8,128)S(1)}) custom-call(f32[6,48,128]{2,1,0:T(8,128)} %state_hbm.1, f32[6,48,128]{2,1,0:T(8,128)} %source_hbm.1, f32[6,48,128]{2,1,0:T(8,128)} %cot_hbm.1, f32[2,48,128]{2,1,0:T(8,128)} %coef_hbm.1, s32[6,48,128]{2,1,0:T(8,128)} %mask_hbm.1, ...), custom_call_target="tpu_custom_call" | custom-call | tf_op jit(solution)/shard_map/window/pallas_call | solution.py:442
  21.7 0.8 %store.1 = (f32[6,48,128]{2,1,0:T(8,128)}, f32[6,48,128]{2,1,0:T(8,128)}, f32[6,48,128]{2,1,0:T(8,128)}) custom-call(f32[6,48,128]{2,1,0:T(8,128)S(1)} %get-tuple-element.6.a_ref, f32[6,48,128]{2,1,0:T(8,128)S(1)} %get-tuple-element.7.b_ref, f32[6,48,128]{2,1,0:T(8,128)S(1)} %get-tuple-element.8.c_ref), custom_call_target="tpu_custom_call" | custom-call | tf_op jit(solution)/shard_map/store/pallas_call | solution.py:466
